TPU v7x, 256 devices: a whole 4x4x8 slice. The times are simulated.
256 devices in a mesh: shot: 64 (over y, x, z_hi), sub: 4 (over z_lo, core).
Axes of the slice: x: 4, y: 4, z: 8 (z_hi: 4, z_lo: 2; z = z_hi * 2 + z_lo), core: 2. Of those that a mesh axis runs over, the one named last changes fastest.
Arguments:
- q_model: float32 [256, 128, 256], P('shot', 'sub'), may hold values from 0.04 to 0.18
- tile_slot: int32 [256], replicated, may hold values from 0 to 255, as said below
- tile_list: int32 [64, 16], replicated, may hold values from 0 to 255, as said below
- rec_index: int32 [64, 256], P('shot'), may hold values from 0 to 524287
- traces: float32 [64, 8, 256], P('shot'), may hold values from -6 to 6
- adj_now: float32 [64, 128, 4096], P('shot', 'sub'), may hold values from -6 to 6
- adj_prev: float32 [64, 128, 4096], P('shot', 'sub'), may hold values from -6 to 6
- fwd_lap: bfloat16 [64, 8, 128, 4096], P('shot', None, 'sub'), may hold values from -0.59765625 to 0.59765625
Outputs:
- gradient: float32 [256, 128, 256], P('shot', 'sub')
- adj_final: bfloat16 [64, 128, 4096], P('shot', 'sub')
Inputs may be any that keep to these rules, and one draw needn't show every extreme that they name: `tile_slot`: A permutation; slots 4 * i to 4 * i + 3 are those of index i of shot. `tile_list`: each row holds 16 distinct tiles. Of one row's tiles at most 2 lie in the slots of one index of shot, and exactly 2 do for some index in every row.
All inputs are finite; a program needn't handle non-finite values.
Results may differ from a plain program's by a relative error of at most 0.001.
Values sent between devices are 32-bit elements; how exact they have to be, the bound alone decides.
A program may use at most 128 MiB of HBM per device.

v0:
```python
import jax
import jax.numpy as jnp
from jax import lax
from jax.sharding import PartitionSpec as P

TS = 16
CAP = 2
AGY = 4


COEFFS = (-205.0 / 72.0, 8.0 / 5.0, -1.0 / 5.0, 8.0 / 315.0, -1.0 / 560.0)


def with_halo(cells, sides, width):
    for axis, dim in sides:
        count = lax.axis_size(axis)
        ends = count - 1
        head = lax.slice_in_dim(cells, 0, width, axis=dim)
        tail = lax.slice_in_dim(cells, cells.shape[dim] - width, cells.shape[dim], axis=dim)
        cells = jnp.concatenate(
            [
                lax.ppermute(tail, axis, [(i, (i + 1) % count) for i in range(ends)]),
                cells,
                lax.ppermute(head, axis, [((i + 1) % count, i) for i in range(ends)]),
            ],
            axis=dim,
        )
    return cells


def laplace(field, width_y):
    depth_dev, plane = field.shape
    margin = 4 * width_y
    stacked = with_halo(field, (("sub", 0),), 4)
    padded = jnp.pad(stacked, ((0, 0), (margin, margin)))
    column_y = jnp.arange(plane, dtype=jnp.int32) % width_y

    def window(shift_z, offset):
        return padded[
            4 + shift_z : 4 + shift_z + depth_dev, margin + offset : margin + offset + plane
        ]

    total = 3.0 * COEFFS[0] * field
    for reach in range(1, 5):
        upper_ok = (column_y + reach < width_y).astype(jnp.float32)
        lower_ok = (column_y - reach >= 0).astype(jnp.float32)
        beside_all = window(reach, 0) + window(-reach, 0)
        beside_all = beside_all + window(0, reach * width_y) + window(0, -reach * width_y)
        beside_all = (
            beside_all
            + upper_ok[None, :] * window(0, reach)
            + lower_ok[None, :] * window(0, -reach)
        )
        total = total + COEFFS[reach] * beside_all
    return total


def routing(tile_slot, tile_list, tiles_dev):
    slots = jnp.take(tile_slot, tile_list, axis=0)
    owners = slots // tiles_dev
    local_slot = slots % tiles_dev
    order = jnp.arange(tile_list.shape[1], dtype=jnp.int32)
    earlier = (owners[:, :, None] == owners[:, None, :]) & (
        order[None, None, :] < order[None, :, None]
    )
    ranks = jnp.sum(earlier.astype(jnp.int32), axis=2)
    return (slots, owners, local_slot, ranks)


def selection(owners, local_slot, ranks, shot_index, tiles_dev):
    mine = owners == shot_index
    hits = (
        mine[:, :, None, None]
        & (ranks[:, :, None, None] == jnp.arange(CAP)[None, None, :, None])
        & (local_slot[:, :, None, None] == jnp.arange(tiles_dev)[None, None, None, :])
    )
    return jnp.sum(hits.astype(jnp.float32), axis=1)


def body(q_model, tile_slot, tile_list, rec_index, traces, adj_now, adj_prev, fwd_lap):
    tiles_dev = q_model.shape[0]
    depth_dev = q_model.shape[1]
    cells = depth_dev * TS * TS
    shots = lax.axis_size("shot")
    blocks = tile_list.shape[1]
    plane = adj_now.shape[2]
    width_y = AGY * TS
    flat_model = q_model.reshape(tiles_dev, cells)
    shot_index = lax.axis_index("shot")
    slots, owners, local_slot, ranks = routing(tile_slot, tile_list, tiles_dev)
    my_slots = lax.dynamic_index_in_dim(slots, shot_index, 0, keepdims=False)
    my_owners = lax.dynamic_index_in_dim(owners, shot_index, 0, keepdims=False)
    my_ranks = lax.dynamic_index_in_dim(ranks, shot_index, 0, keepdims=False)
    piece = lax.all_gather(flat_model, "shot", axis=0, tiled=True)
    count = piece.shape[0]
    valid = (my_slots >= 0) & (my_slots < count)
    rows = jnp.take(piece, jnp.clip(my_slots, 0, count - 1), axis=0)
    tiles = jnp.where(valid[:, None], rows, 0.0)
    blocks_x = blocks // AGY
    speed = (
        tiles.reshape(blocks_x, AGY, depth_dev, TS, TS)
        .transpose(2, 0, 3, 1, 4)
        .reshape(depth_dev, plane)
    )
    depth_start = lax.axis_index("sub") * depth_dev
    receivers = rec_index[0]
    column = receivers % plane
    level = receivers // plane - depth_start
    inside = (level >= 0) & (level < depth_dev)
    volume = depth_dev * plane
    target = jnp.where(inside, level * plane + column, volume)
    current = adj_now[0]
    previous = adj_prev[0]
    image = jnp.zeros((depth_dev, plane), jnp.float32)
    for step in range(fwd_lap.shape[1]):
        source = (
            jnp.zeros((volume,), jnp.float32)
            .at[target]
            .add(traces[0, step], mode="drop")
            .reshape(depth_dev, plane)
        )
        updated = 2.0 * current - previous + speed * laplace(current, width_y) + source
        image = image + fwd_lap[0, step].astype(jnp.float32) * updated
        previous = current
        current = updated
    grad_tiles = (
        image.reshape(depth_dev, blocks_x, TS, AGY, TS)
        .transpose(1, 3, 0, 2, 4)
        .reshape(blocks, cells)
    )
    extended = jnp.concatenate([grad_tiles, jnp.zeros((1, cells), jnp.float32)], axis=0)
    select_back = selection(owners, local_slot, ranks, shot_index, tiles_dev)
    placement = (
        jnp.full((shots * CAP,), blocks, jnp.int32)
        .at[my_owners * CAP + my_ranks]
        .set(jnp.arange(blocks, dtype=jnp.int32))
    )
    outgoing_grad = jnp.take(extended, placement, axis=0).reshape(shots, CAP, cells)
    incoming_grad = lax.all_to_all(outgoing_grad, "shot", split_axis=0, concat_axis=0, tiled=True)
    summed = jnp.einsum("rcs,rck->sk", select_back, incoming_grad, precision=lax.Precision.HIGHEST)
    return (summed.reshape(q_model.shape), current.astype(jnp.bfloat16)[None])


def solution(mesh):
    in_specs = (
        P("shot", "sub", None),
        P(),
        P(),
        P("shot", None),
        P("shot", None, None),
        P("shot", "sub", None),
        P("shot", "sub", None),
        P("shot", None, "sub", None),
    )
    out_specs = (P("shot", "sub", None), P("shot", "sub", None))
    return jax.shard_map(body, mesh=mesh, in_specs=in_specs, out_specs=out_specs, check_vma=False)
```

profile of v0, /device:TPU:1, one launch (start us, length us, event | category | flops | bytes accessed | tf_op | source)
XLA Modules:
  0.0 728.3 jit_solution(16691050275457656651)
XLA Ops:
  9.9 5.1 collective-permute-start
  16.9 3.0 copy.210
  20.1 6.9 gather_fusion
  39.9 4.0 select_maximum_fusion.14
  43.9 79.0 %all-gather.3.cloned.1.call-done = f32[64,4,8192]{2,1,0:T(4,128)} async-done(((f32[1,4,8192]{2,1,0:T(4,128)}), f32[64,4,8192]{2,1,0:T(4,128)}) %all-gather.3.cloned.1.call-update) | async-done | bytes 8388624 | tf_op jit(solution)/shard_map/all_gather | solution.py:94
  122.9 10.0 %reshape.567 = f32[256,8192]{1,0:T(8,128)} reshape(f32[64,4,8192]{2,1,0:T(4,128)} %all-gather.3.cloned.1.call-done) | data formatting | bytes 16777216
  132.9 4.3 gather_fusion.1
  140.0 4.8 select_bitcast_fusion
  144.8 4.2 copy.212
  149.1 26.8 %fusion.183 = f32[32,4096]{0,1:T(8,128)S(1)} fusion(f32[32,4096]{0,1:T(8,128)} %copy.217, f32[40,4608]{0,1:T(8,128)S(1)} %select_maximum_fusion.14, f32[32,4096]{0,1:T(8,128)} %bitcast.95, f32[4,4096]{0,1:T(8,128)} %copy.214, f32[4,4096]{0,1:T(8,128)} %copy.213, f32[32,4,16,4,16]{0,4,3,2,1:T(8,128)} %copy.212, f32[1,32,4096]{1,2,0:T(8,128)} %copy.211, ...), kind=kLoop, calls=%fused_computation.370 | loop fusion | flops 6553600 | bytes 11272192 | tf_op jit(solution)/shard_map/add | solution.py:122
  180.2 10.4 %collective-permute-start.2 = (f32[4,4096]{1,0:T(4,128)S(1)}, f32[4,4096]{1,0:T(4,128)S(1)}, u32[]{:S(2)}, u32[]{:S(2)}) collective-permute-start(f32[4,4096]{1,0:T(4,128)S(1)} %copy.219), channel_id=1, source_target_pairs={{1,0},{2,1},{3,2},{5,4},{6,5},{7,6},{9,8},{10,9},{11,10},{13,12},{... | collective-permute-start | bytes 196616 | tf_op jit(solution)/shard_map/ppermute | solution.py:24
  202.0 4.2 select_maximum_fusion.12
  207.3 24.7 %fusion.158 = f32[32,4096]{0,1:T(8,128)S(1)} fusion(f32[32,4096]{0,1:T(8,128)} %copy.225, f32[40,4608]{0,1:T(8,128)S(1)} %select_maximum_fusion.12, f32[32,4096]{0,1:T(8,128)S(1)} %copy-done.4, f32[4,4096]{0,1:T(8,128)} %copy.222, f32[4,4096]{0,1:T(8,128)S(1)} %copy-done.26, f32[32,4,16,4,16]{0,4,3,2,1:T(8,128)S(1)} %copy-done.2, ...), kind=kLoop, calls=%fused_computation.323 | loop fusion | flops 6553600 | bytes 11272192 | tf_op jit(solution)/shard_map/add | solution.py:122
  241.1 3.6 collective-permute-start.5
  253.2 4.2 select_maximum_fusion.10
  258.5 23.8 %fusion.133 = f32[32,4096]{0,1:T(8,128)S(1)} fusion(f32[32,4096]{0,1:T(8,128)} %copy.233, f32[40,4608]{0,1:T(8,128)S(1)} %select_maximum_fusion.10, f32[32,4096]{0,1:T(8,128)S(1)} %copy-done.7, f32[4,4096]{0,1:T(8,128)S(1)} %copy-done.32, f32[4,4096]{0,1:T(8,128)S(1)} %copy-done.27, f32[32,4,16,4,16]{0,4,3,2,1:T(8,128)S(1)} %copy-done.2, ...), kind=kLoop, calls=%fused_computation.276 | loop fusion | flops 6553600 | bytes 11272192 | tf_op jit(solution)/shard_map/add | solution.py:122
  285.1 2.8 copy.235
  292.7 3.6 collective-permute-start.7
  306.2 2.9 copy.238
  309.1 4.2 select_maximum_fusion.8
  314.4 23.8 %fusion.108 = f32[32,4096]{0,1:T(8,128)S(1)} fusion(f32[32,4096]{0,1:T(8,128)} %copy.241, f32[40,4608]{0,1:T(8,128)S(1)} %select_maximum_fusion.8, f32[32,4096]{0,1:T(8,128)S(1)} %copy-done.10, f32[4,4096]{0,1:T(8,128)S(1)} %copy-done.33, f32[4,4096]{0,1:T(8,128)S(1)} %copy-done.28, f32[32,4,16,4,16]{0,4,3,2,1:T(8,128)S(1)} %copy-done.2, ...), kind=kLoop, calls=%fused_computation.229 | loop fusion | flops 6553600 | bytes 11272192 | tf_op jit(solution)/shard_map/add | solution.py:122
  341.0 2.8 copy.243
  345.7 2.8 copy.245
  348.6 3.8 collective-permute-start.9
  358.0 2.9 copy.244
  363.7 4.2 select_maximum_fusion.6
  369.0 23.8 %fusion.83 = f32[32,4096]{0,1:T(8,128)S(1)} fusion(f32[32,4096]{0,1:T(8,128)} %copy.249, f32[40,4608]{0,1:T(8,128)S(1)} %select_maximum_fusion.6, f32[32,4096]{0,1:T(8,128)S(1)} %copy-done.13, f32[4,4096]{0,1:T(8,128)S(1)} %copy-done.34, f32[4,4096]{0,1:T(8,128)S(1)} %copy-done.29, f32[32,4,16,4,16]{0,4,3,2,1:T(8,128)S(1)} %copy-done.2, ...), kind=kLoop, calls=%fused_computation.182 | loop fusion | flops 6553600 | bytes 11272192 | tf_op jit(solution)/shard_map/add | solution.py:122
  403.1 3.6 collective-permute-start.11
  417.5 4.2 select_maximum_fusion.4
  422.8 23.8 %fusion.58 = f32[32,4096]{0,1:T(8,128)S(1)} fusion(f32[32,4096]{0,1:T(8,128)} %copy.257, f32[40,4608]{0,1:T(8,128)S(1)} %select_maximum_fusion.4, f32[32,4096]{0,1:T(8,128)S(1)} %copy-done.16, f32[4,4096]{0,1:T(8,128)S(1)} %copy-done.35, f32[4,4096]{0,1:T(8,128)S(1)} %copy-done.30, f32[32,4,16,4,16]{0,4,3,2,1:T(8,128)S(1)} %copy-done.2, ...), kind=kLoop, calls=%fused_computation.135 | loop fusion | flops 6553600 | bytes 11272192 | tf_op jit(solution)/shard_map/add | solution.py:122
  449.2 2.8 copy.259
  456.8 3.6 collective-permute-start.13
  484.2 2.8 copy.262
  487.0 4.2 select_maximum_fusion.2
  492.3 23.8 %fusion.33 = f32[32,4096]{0,1:T(8,128)S(1)} fusion(f32[32,4096]{0,1:T(8,128)} %copy.265, f32[40,4608]{0,1:T(8,128)S(1)} %select_maximum_fusion.2, f32[32,4096]{0,1:T(8,128)S(1)} %copy-done.19, f32[4,4096]{0,1:T(8,128)S(1)} %copy-done.36, f32[4,4096]{0,1:T(8,128)S(1)} %copy-done.31, f32[32,4,16,4,16]{0,4,3,2,1:T(8,128)S(1)} %copy-done.2, ...), kind=kLoop, calls=%fused_computation.88 | loop fusion | flops 6553600 | bytes 11272192 | tf_op jit(solution)/shard_map/add | solution.py:122
  525.2 3.8 collective-permute-start.15
  533.0 4.2 select_maximum_fusion
  538.4 24.7 %convert_bitcast_fusion = (bf16[1,32,4096]{1,2,0:T(8,128)(2,1)S(1)}, f32[32,4096]{0,1:T(8,128)}) fusion(f32[32,4096]{0,1:T(8,128)} %copy.273, f32[40,4608]{0,1:T(8,128)S(1)} %select_maximum_fusion, f32[4096]{0:T(1024)S(1)} %get-tuple-element.58, f32[4096]{0:T(1024)S(1)} %get-tuple-element.57, f32[32,4096]{0,1:T(8,128)S(1)} %copy-done.22, ...), kind=kLoop, calls=%fused_computation.428 | loop fusion | flops 6684672 | bytes 11534336 | tf_op jit(solution)/shard_map/broadcast_in_dim | solution.py:141
  563.0 9.7 %fusion.203 = f32[32,4096]{0,1:T(8,128)S(1)} fusion(f32[32,4096]{0,1:T(8,128)} %get-tuple-element.13, f32[32,4096]{0,1:T(8,128)} %copy-done.21, f32[32,4096]{0,1:T(8,128)} %copy-done.18, f32[32,4096]{0,1:T(8,128)} %copy-done.15, f32[32,4096]{0,1:T(8,128)} %copy-done.12, f32[32,4096]{0,1:T(8,128)} %copy-done.9, f32[32,4096]{0,1:T(8,128)} %copy-done.6, ...), kind=kLoop, calls=%fused_computation.412 | loop fusion | flops 3014656 | bytes 6815744 | tf_op jit(solution)/shard_map/add | solution.py:123
  572.8 3.0 copy.274
  575.8 4.7 reshape.458
  580.6 3.7 gather_fusion.2
  584.3 5.9 gather.20
  590.2 7.9 %broadcast_select_fusion = f32[64,2,8192]{2,1,0:T(2,128)} fusion(f32[64,2,8192]{2,1,0:T(2,128)} %gather.20, pred[64,2]{1,0:T(8,128)(4,1)S(1)} %broadcast_in_dim.52), kind=kLoop, calls=%fused_computation.15 | loop fusion | flops 1048576 | bytes 8388736 | tf_op jit(solution)/shard_map/jit(_take)/select_n | solution.py:138
  598.1 10.3 %all-to-all-start = ((f32[64,2,8192]{2,1,0:T(2,128)}), f32[64,2,8192]{2,1,0:T(2,128)}, u32[]{:S(2)}, u32[]{:S(2)}) async-start(f32[64,2,8192]{2,1,0:T(2,128)} %broadcast_select_fusion), calls=%async_computation | async-start | bytes 8388608 | tf_op jit(solution)/shard_map/all_to_all | solution.py:139
  609.6 97.8 %all-to-all-done = f32[64,2,8192]{2,1,0:T(2,128)} async-done(((f32[64,2,8192]{2,1,0:T(2,128)}), f32[64,2,8192]{2,1,0:T(2,128)}, u32[]{:S(2)}, u32[]{:S(2)}) %all-to-all-start) | async-done | bytes 4194336 | tf_op jit(solution)/shard_map/all_to_all | solution.py:139
  707.4 6.7 reshape.571
  714.1 6.4 fusion.210
  (243 shorter events, 158.6 us)
Async XLA Ops:
  7.2 12.9 %copy-start = (s32[256]{0:T(256)S(1)}, s32[256]{0:T(256)}, u32[]{:S(2)}) copy-start(s32[256]{0:T(256)} %param.9) | copy-start | bytes 3076
  7.2 12.7 %copy-start.48 = (s32[64,16]{0,1:T(8,128)S(1)}, s32[64,16]{0,1:T(8,128)}, u32[]{:S(2)}) copy-start(s32[64,16]{0,1:T(8,128)} %param.10) | copy-start | bytes 12292
  7.2 115.7 %all-gather.3.cloned.1.call-start = ((), (), s32[]{:S(2)}) async-start(), calls=%async_computation.1 | async-start | bytes 8519680 | tf_op jit(solution)/shard_map/all_gather | solution.py:94
  9.9 26.0 %collective-permute-start = (f32[4,4096]{1,0:T(4,128)S(1)}, f32[4,4096]{1,0:T(4,128)S(1)}, u32[]{:S(2)}, u32[]{:S(2)}) collective-permute-start(f32[4,4096]{1,0:T(4,128)S(1)} %get-tuple-element.40), channel_id=1, source_target_pairs={{1,0},{2,1},{3,2},{5,4},{6,5},{7,6},{9,8},{10,9},{11,10},{13,12},{... | collective-permute-start | bytes 196616 | tf_op jit(solution)/shard_map/ppermute | solution.py:24
  15.0 22.9 %collective-permute-start.1 = (f32[4,4096]{1,0:T(4,128)S(1)}, f32[4,4096]{1,0:T(4,128)S(1)}, u32[]{:S(2)}, u32[]{:S(2)}) collective-permute-start(f32[4,4096]{1,0:T(4,128)S(1)} %get-tuple-element.39), channel_id=1, source_target_pairs={{0,1},{1,2},{2,3},{4,5},{5,6},{6,7},{8,9},{9,10},{10,11},{12,13},{... | collective-permute-start | bytes 196616 | tf_op jit(solution)/shard_map/ppermute | solution.py:22
  20.1 8.9 %copy-start.51 = (s32[1,256]{1,0:T(1,128)S(1)}, s32[1,256]{1,0:T(1,128)}, u32[]{:S(2)}) copy-start(s32[1,256]{1,0:T(1,128)} %param.11) | copy-start | bytes 3076
  20.1 8.9 %copy-start.50 = (f32[1,8,256]{2,1,0:T(8,128)S(1)}, f32[1,8,256]{2,1,0:T(8,128)}, u32[]{:S(2)}) copy-start(f32[1,8,256]{2,1,0:T(8,128)} %param.12) | copy-start | bytes 24580
  29.0 164.8 %copy-start.52 = (s32[256,1]{0,1:T(1,128)}, s32[256,1]{0,1:T(1,128)S(1)}, u32[]{:S(2)}) copy-start(s32[256,1]{0,1:T(1,128)S(1)} %compare_select_fusion.1) | copy-start | bytes 3076
  180.2 17.8 %collective-permute-start.2 = (f32[4,4096]{1,0:T(4,128)S(1)}, f32[4,4096]{1,0:T(4,128)S(1)}, u32[]{:S(2)}, u32[]{:S(2)}) collective-permute-start(f32[4,4096]{1,0:T(4,128)S(1)} %copy.219), channel_id=1, source_target_pairs={{1,0},{2,1},{3,2},{5,4},{6,5},{7,6},{9,8},{10,9},{11,10},{13,12},{... | collective-permute-start | bytes 196616 | tf_op jit(solution)/shard_map/ppermute | solution.py:24
  191.2 8.8 %collective-permute-start.3 = (f32[4,4096]{1,0:T(4,128)S(1)}, f32[4,4096]{1,0:T(4,128)S(1)}, u32[]{:S(2)}, u32[]{:S(2)}) collective-permute-start(f32[4,4096]{1,0:T(4,128)S(1)} %copy.221), channel_id=1, source_target_pairs={{0,1},{1,2},{2,3},{4,5},{5,6},{6,7},{8,9},{9,10},{10,11},{12,13},{... | collective-permute-start | bytes 196616 | tf_op jit(solution)/shard_map/ppermute | solution.py:22
  202.0 4.7 copy-start.23
  202.0 5.3 copy-start.26
  236.9 12.3 %collective-permute-start.4 = (f32[4,4096]{1,0:T(4,128)S(1)}, f32[4,4096]{1,0:T(4,128)S(1)}, u32[]{:S(2)}, u32[]{:S(2)}) collective-permute-start(f32[4,4096]{1,0:T(4,128)S(1)} %copy.227), channel_id=1, source_target_pairs={{1,0},{2,1},{3,2},{5,4},{6,5},{7,6},{9,8},{10,9},{11,10},{13,12},{... | collective-permute-start | bytes 196616 | tf_op jit(solution)/shard_map/ppermute | solution.py:24
  241.1 10.2 %collective-permute-start.5 = (f32[4,4096]{1,0:T(4,128)S(1)}, f32[4,4096]{1,0:T(4,128)S(1)}, u32[]{:S(2)}, u32[]{:S(2)}) collective-permute-start(f32[4,4096]{1,0:T(4,128)S(1)} %copy.229), channel_id=1, source_target_pairs={{0,1},{1,2},{2,3},{4,5},{5,6},{6,7},{8,9},{9,10},{10,11},{12,13},{... | collective-permute-start | bytes 196616 | tf_op jit(solution)/shard_map/ppermute | solution.py:22
  253.2 4.7 copy-start.27
  253.2 5.3 copy-start.32
  287.9 15.5 %collective-permute-start.6 = (f32[4,4096]{1,0:T(4,128)}, f32[4,4096]{1,0:T(4,128)}, u32[]{:S(2)}, u32[]{:S(2)}) collective-permute-start(f32[4,4096]{1,0:T(4,128)} %copy.235), channel_id=1, source_target_pairs={{1,0},{2,1},{3,2},{5,4},{6,5},{7,6},{9,8},{10,9},{11,10},{13,12},{... | collective-permute-start | bytes 196616 | tf_op jit(solution)/shard_map/ppermute | solution.py:24
  292.7 13.5 %collective-permute-start.7 = (f32[4,4096]{1,0:T(4,128)}, f32[4,4096]{1,0:T(4,128)}, u32[]{:S(2)}, u32[]{:S(2)}) collective-permute-start(f32[4,4096]{1,0:T(4,128)} %copy.237), channel_id=1, source_target_pairs={{0,1},{1,2},{2,3},{4,5},{5,6},{6,7},{8,9},{9,10},{10,11},{12,13},{... | collective-permute-start | bytes 196616 | tf_op jit(solution)/shard_map/ppermute | solution.py:22
  309.1 4.7 copy-start.28
  309.1 5.3 copy-start.33
  341.0 11.5 %copy-start.53 = (s32[16]{0:T(128)S(1)}, s32[16]{0:T(128)}, u32[]{:S(2)}) copy-start(s32[16]{0:T(128)} %get-tuple-element.50) | copy-start | bytes 196
  343.8 14.2 %collective-permute-start.8 = (f32[4,4096]{1,0:T(4,128)}, f32[4,4096]{1,0:T(4,128)}, u32[]{:S(2)}, u32[]{:S(2)}) collective-permute-start(f32[4,4096]{1,0:T(4,128)} %copy.243), channel_id=1, source_target_pairs={{1,0},{2,1},{3,2},{5,4},{6,5},{7,6},{9,8},{10,9},{11,10},{13,12},{... | collective-permute-start | bytes 196616 | tf_op jit(solution)/shard_map/ppermute | solution.py:24
  348.6 12.3 %collective-permute-start.9 = (f32[4,4096]{1,0:T(4,128)}, f32[4,4096]{1,0:T(4,128)}, u32[]{:S(2)}, u32[]{:S(2)}) collective-permute-start(f32[4,4096]{1,0:T(4,128)} %copy.245), channel_id=1, source_target_pairs={{0,1},{1,2},{2,3},{4,5},{5,6},{6,7},{8,9},{9,10},{10,11},{12,13},{... | collective-permute-start | bytes 196616 | tf_op jit(solution)/shard_map/ppermute | solution.py:22
  358.0 48.8 %copy-start.55 = (s32[128]{0:T(128)}, s32[128]{0:T(128)S(1)}, u32[]{:S(2)}) copy-start(s32[128]{0:T(128)S(1)} %scatter_custom_fusion) | copy-start | bytes 1540
  363.7 4.7 copy-start.29
  363.7 5.3 copy-start.34
  398.4 13.5 %collective-permute-start.10 = (f32[4,4096]{1,0:T(4,128)}, f32[4,4096]{1,0:T(4,128)}, u32[]{:S(2)}, u32[]{:S(2)}) collective-permute-start(f32[4,4096]{1,0:T(4,128)} %copy.251), channel_id=1, source_target_pairs={{1,0},{2,1},{3,2},{5,4},{6,5},{7,6},{9,8},{10,9},{11,10},{13,12},{... | collective-permute-start | bytes 196616 | tf_op jit(solution)/shard_map/ppermute | solution.py:24
  403.1 11.5 %collective-permute-start.11 = (f32[4,4096]{1,0:T(4,128)}, f32[4,4096]{1,0:T(4,128)}, u32[]{:S(2)}, u32[]{:S(2)}) collective-permute-start(f32[4,4096]{1,0:T(4,128)} %copy.253), channel_id=1, source_target_pairs={{0,1},{1,2},{2,3},{4,5},{5,6},{6,7},{8,9},{9,10},{10,11},{12,13},{... | collective-permute-start | bytes 196616 | tf_op jit(solution)/shard_map/ppermute | solution.py:22
  417.4 4.7 copy-start.30
  417.4 5.3 copy-start.35
  449.2 11.2 %copy-start.56 = (s32[128]{0:T(128)S(1)}, s32[128]{0:T(128)}, u32[]{:S(2)}) copy-start(s32[128]{0:T(128)} %copy-done.55) | copy-start | bytes 1540
  452.1 29.2 %collective-permute-start.12 = (f32[4,4096]{1,0:T(4,128)}, f32[4,4096]{1,0:T(4,128)}, u32[]{:S(2)}, u32[]{:S(2)}) collective-permute-start(f32[4,4096]{1,0:T(4,128)} %copy.259), channel_id=1, source_target_pairs={{1,0},{2,1},{3,2},{5,4},{6,5},{7,6},{9,8},{10,9},{11,10},{13,12},{... | collective-permute-start | bytes 196616 | tf_op jit(solution)/shard_map/ppermute | solution.py:24
  456.8 27.3 %collective-permute-start.13 = (f32[4,4096]{1,0:T(4,128)}, f32[4,4096]{1,0:T(4,128)}, u32[]{:S(2)}, u32[]{:S(2)}) collective-permute-start(f32[4,4096]{1,0:T(4,128)} %copy.261), channel_id=1, source_target_pairs={{0,1},{1,2},{2,3},{4,5},{5,6},{6,7},{8,9},{9,10},{10,11},{12,13},{... | collective-permute-start | bytes 196616 | tf_op jit(solution)/shard_map/ppermute | solution.py:22
  469.5 5.0 copy-start.40
  470.8 5.0 copy-start.39
  487.0 4.7 copy-start.31
  487.0 5.3 copy-start.36
  518.8 10.2 %copy-start.54 = (s32[128]{0:T(128)S(1)}, s32[128]{0:T(128)}, u32[]{:S(2)}) copy-start(s32[128]{0:T(128)} %compare_select_fusion.4) | copy-start | bytes 1540
  521.0 8.0 %collective-permute-start.14 = (f32[4,4096]{1,0:T(4,128)S(1)}, f32[4,4096]{1,0:T(4,128)S(1)}, u32[]{:S(2)}, u32[]{:S(2)}) collective-permute-start(f32[4,4096]{1,0:T(4,128)S(1)} %copy.267), channel_id=1, source_target_pairs={{1,0},{2,1},{3,2},{5,4},{6,5},{7,6},{9,8},{10,9},{11,10},{13,12},{... | collective-permute-start | bytes 196616 | tf_op jit(solution)/shard_map/ppermute | solution.py:24
  525.2 5.9 collective-permute-start.15
  533.0 4.2 copy-start.22
  533.0 4.7 copy-start.24
  533.0 5.3 copy-start.25
  598.1 10.3 %copy-start.47 = (s32[64,16]{0,1:T(8,128)S(1)}, s32[64,16]{0,1:T(8,128)}, u32[]{:S(2)}) copy-start(s32[64,16]{0,1:T(8,128)} %copy-done.46) | copy-start | bytes 12292
  598.1 10.3 %copy-start.49 = (pred[64,16]{0,1:T(8,128)(4,1)S(1)}, pred[64,16]{0,1:T(8,128)(4,1)}, u32[]{:S(2)}) copy-start(pred[64,16]{0,1:T(8,128)(4,1)} %get-tuple-element.14) | copy-start | bytes 3076
  598.1 10.3 %copy-start.45 = (s32[64,16]{0,1:T(8,128)S(1)}, s32[64,16]{0,1:T(8,128)}, u32[]{:S(2)}) copy-start(s32[64,16]{0,1:T(8,128)} %copy-done.44) | copy-start | bytes 12292
  598.1 109.2 %all-to-all-start = ((f32[64,2,8192]{2,1,0:T(2,128)}), f32[64,2,8192]{2,1,0:T(2,128)}, u32[]{:S(2)}, u32[]{:S(2)}) async-start(f32[64,2,8192]{2,1,0:T(2,128)} %broadcast_select_fusion), calls=%async_computation | async-start | bytes 8388608 | tf_op jit(solution)/shard_map/all_to_all | solution.py:139
  707.4 13.8 %copy-start.1 = (s32[256]{0:T(256)S(1)}, s32[256]{0:T(256)}, u32[]{:S(2)}) copy-start(s32[256]{0:T(256)} %param.9) | copy-start | bytes 3076
  (27 other events, 92.9 us)
Sparse Core Ops, SparseCore 0:
  11.9 110.9 all-gather.2
where the time goes:
time: 739 us; the launch traced here: 728 us
  other arithmetic  272 us (37%)
  local copies, waits for them, and re-layouts  194 us (26%)
  waiting for transfers between devices  177 us (24%)
  starting transfers between devices  64 us (9%)
  between operations  15.2 us (2%)
    add x7, other arithmetic, body(): 2.0 * current - previous + speed * laplace(current, width_y) + source  171 us
    all_to_all x1, waiting for transfers between devices, body(): lax.all_to_all(outgoing_grad, 'shot', split_axis=0, concat_axis=0, tiled=...  97.8 us
    all_gather x1, waiting for transfers between devices, body(): piece = lax.all_gather(flat_model, 'shot', axis=0, tiled=True)  79 us
    unnamed x128, local copies, waits for them, and re-layouts  38.2 us
    slice x15, local copies, waits for them, and re-layouts, with_halo(): lax.slice_in_dim(cells, cells.shape[dim] - width, cells.shape[dim], axis=...  35.5 us
    concatenate x8, other arithmetic, with_halo(): jnp.concatenate([lax.ppermute(tail, axis, [(i, (i + 1) % count) for i in...  33.1 us
    ppermute x8, starting transfers between devices, with_halo(): lax.ppermute(head, axis, [((i + 1) % count, i) for i in range(ends)])  27 us
    ppermute x8, starting transfers between devices, with_halo(): lax.ppermute(tail, axis, [(i, (i + 1) % count) for i in range(ends)])  26.7 us
  transfers between devices with their start and end apart: 18, of which 2 were waited for; matrix products, arithmetic and copies ran while one was open for 15% of the time, Pallas kernels for 0%

commit v1 on v0

v1 whole, which is shorter than its diff:
```python
import functools

import jax
import jax.numpy as jnp
import numpy as np
from jax import lax
from jax.experimental import pallas as pl
from jax.experimental.pallas import tpu as pltpu
from jax.sharding import PartitionSpec as P

TS = 16
STEPS = 8
ROWS = 32
LANES = 256
PLANE = 4096
COEFFS = (-205.0 / 72.0, 8.0 / 5.0, -1.0 / 5.0, 8.0 / 315.0, -1.0 / 560.0)
C1 = COEFFS[1]
REL = tuple(c / C1 for c in COEFFS)

NCH = 2
R = ROWS // NCH

MESH = pl.DeviceIdType.MESH
VMEM_LIMIT = 60 * 1024 * 1024
F32 = jnp.float32
BF16 = jnp.bfloat16


def lateral_matrices():
    out = np.zeros((3, LANES, LANES), np.float32)
    k = np.arange(LANES)[:, None]
    n = np.arange(LANES)[None, :]
    for d in (-1, 0, 1):
        dx = 4 * d + k // 64 - n // 64
        dy = k % 64 - n % 64
        for reach in range(1, 5):
            hit = ((dx == 0) & (np.abs(dy) == reach)) | ((dy == 0) & (np.abs(dx) == reach))
            out[d + 1][hit] = REL[reach]
    return out


def coords():
    me = lax.axis_index("shot")
    return me // 16, (me // 4) % 4, me % 4


def shot_at(y, x, z):
    return (y * 4 + x) * 4 + z


class Links:
    def __init__(self):
        self.y, self.x, self.z = coords()
        self.sub = lax.axis_index("sub")

    def step(self, axis, delta):
        y, x, z = self.y, self.x, self.z
        if axis == "y":
            y = (y + delta + 4) % 4
        elif axis == "x":
            x = (x + delta + 4) % 4
        else:
            z = (z + delta + 4) % 4
        return shot_at(y, x, z)

    def barrier(self):
        sem = pltpu.get_barrier_semaphore()
        for axis in ("y", "x", "z"):
            for delta in (1, -1):
                pl.semaphore_signal(
                    sem, inc=1, device_id=(self.step(axis, delta), self.sub), device_id_type=MESH
                )
        pl.semaphore_wait(sem, 6)


def ring(v):
    return (v + 8) % 4


def rcopy(links, axis, delta, src, dst, ssem, rsem, c, k):
    return pltpu.make_async_remote_copy(
        src_ref=src,
        dst_ref=dst,
        send_sem=ssem.at[c, k],
        recv_sem=rsem.at[c, k],
        device_id=(links.step(axis, delta), links.sub),
        device_id_type=MESH,
    )


def axes_of(c):
    return ("x", "y") if c % 2 == 0 else ("y", "x")


def slot_parts(slot, order):
    if order == 0:
        return slot // 64, slot % 64
    return (slot // 4) // 4 % 4, (slot // 64) * 16 + slot % 16


def gather_kernel(ts, tl, q_ref, out_ref, *scratch):
    g = scratch[:NCH]
    rel_s = scratch[NCH : 2 * NCH]
    rel_r = scratch[2 * NCH : 3 * NCH]
    blk_s = scratch[3 * NCH : 4 * NCH]
    blk_r = scratch[4 * NCH : 5 * NCH]
    ssem, rsem = scratch[5 * NCH], scratch[5 * NCH + 1]
    links = Links()
    here = {"y": links.y, "x": links.x, "z": links.z}
    z = links.z
    links.barrier()
    sent = []

    def go(copy):
        copy.start()
        sent.append(copy)
        return copy

    def rows(c):
        return pl.ds(c * R, R)

    def part(line, zz, t0=0, n=4):
        return pl.ds(line * 16 + zz * 4 + t0, n)

    p1, p2 = {}, {}
    for c in range(NCH):
        line = here[axes_of(c)[0]]
        src = q_ref.at[:, rows(c)]
        for d, delta in enumerate((1, -1)):
            p1[c, d] = go(rcopy(links, "z", delta, src, g[c].at[part(line, z)], ssem, rsem, c, d))
    for c in range(NCH):
        line = here[axes_of(c)[0]]
        for t in range(4):
            g[c][line * 16 + z * 4 + t] = q_ref[t, c * R : (c + 1) * R, :]
    for c in range(NCH):
        line = here[axes_of(c)[0]]
        for d, delta in enumerate((1, -1)):
            p1[c, d].wait_recv()
            piece = g[c].at[part(line, ring(z - delta), 2 * d, 2)]
            p2[c, d] = go(rcopy(links, "z", delta, piece, piece, ssem, rsem, c, 2 + d))
    a1, a2 = {}, {}
    for c in range(NCH):
        axis = axes_of(c)[0]
        line = here[axis]
        for d in range(2):
            p2[c, d].wait_recv()
        block = g[c].at[pl.ds(line * 16, 16)]
        for d, delta in enumerate((1, -1)):
            a1[c, d] = go(rcopy(links, axis, delta, block, block, ssem, rsem, c, 4 + d))
    for c in range(NCH):
        axis = axes_of(c)[0]
        line = here[axis]
        for d, delta in enumerate((1, -1)):
            a1[c, d].wait_recv()
            piece = g[c].at[pl.ds(ring(line - delta) * 16 + 8 * d, 8)]
            a2[c, d] = go(rcopy(links, axis, delta, piece, piece, ssem, rsem, c, 6 + d))

    def target(c, delta, p):
        last = axes_of(c)[1]
        slot = ts[tl[links.step(last, delta), p]]
        return slot_parts(slot, c % 2)

    rl, bl = {}, {}
    for c in range(NCH):
        last = axes_of(c)[1]
        for d in range(2):
            a2[c, d].wait_recv()
        for d, delta in enumerate((1, -1)):
            for p in range(8):
                _, at = target(c, 2, 8 * d + p)
                rel_s[c][d, p] = g[c][at]
            rl[c, d] = go(
                rcopy(links, last, delta, rel_s[c].at[d], rel_r[c].at[d], ssem, rsem, c, 8 + d)
            )
    for c in range(NCH):
        last = axes_of(c)[1]
        mine = here[last]
        for d, delta in enumerate((1, -1)):
            rl[c, d].wait_recv()
            for p in range(16):
                owner, at = target(c, delta, p)
                value = g[c][at]
                if p // 8 == d:
                    value = jnp.where(owner == mine, value, rel_r[c][d, p % 8])
                blk_s[c][d, p] = value
            bl[c, d] = go(
                rcopy(links, last, delta, blk_s[c].at[d], blk_r[c].at[d], ssem, rsem, c, 10 + d)
            )
    for c in range(NCH):
        mine = here[axes_of(c)[1]]
        for d in range(2):
            bl[c, d].wait_recv()
        for p in range(16):
            owner, at = target(c, 0, p)
            gap = ring(owner - mine)
            if p < 8:
                other = jnp.where(gap == 1, blk_r[c][1, p], blk_r[c][0, p])
            else:
                other = jnp.where(gap == 3, blk_r[c][0, p], blk_r[c][1, p])
            out_ref[p, c * R : (c + 1) * R, :] = jnp.where(gap == 0, g[c][at], other)
    for copy in sent:
        copy.wait_send()


def gather_tiles(tile_slot, tile_list, q_model):
    smem = pl.BlockSpec(memory_space=pltpu.SMEM)
    vmem = pl.BlockSpec(memory_space=pltpu.VMEM)
    scratch = (
        [pltpu.VMEM((64, R, LANES), F32)] * NCH
        + [pltpu.VMEM((2, 8, R, LANES), F32)] * (2 * NCH)
        + [pltpu.VMEM((2, 16, R, LANES), F32)] * (2 * NCH)
        + [pltpu.SemaphoreType.DMA((NCH, 12))] * 2
    )
    return pl.pallas_call(
        gather_kernel,
        out_shape=jax.ShapeDtypeStruct((16, ROWS, LANES), F32),
        in_specs=[smem, smem, vmem],
        out_specs=vmem,
        scratch_shapes=scratch,
        compiler_params=pltpu.CompilerParams(
            collective_id=0, has_side_effects=True, vmem_limit_bytes=VMEM_LIMIT
        ),
    )(tile_slot, tile_list, q_model)


def split2(v):
    hi = v.astype(BF16)
    return hi, (v - hi.astype(F32)).astype(BF16)


def split3(v):
    hi = v.astype(BF16)
    rest = v - hi.astype(F32)
    mid = rest.astype(BF16)
    return hi, mid, (rest - mid.astype(F32)).astype(BF16)


def dot(a, b, transposed=False):
    dims = (((1,), (1,)), ((), ())) if transposed else (((1,), (0,)), ((), ()))
    return lax.dot_general(a, b, dims, preferred_element_type=F32)


def steps_kernel(
    rec, tr, u_in, w_in, fwd, qt, mats, gt_out, fin_out,
    U, H, LO, Q, G, S, PM, T3, hs, hr, ssem, rsem,
):
    shot, sub = lax.axis_index("shot"), lax.axis_index("sub")
    has_up, has_dn = sub > 0, sub < 3
    sides = ((has_up, sub - 1), (has_dn, sub + 1))
    sem = pltpu.get_barrier_semaphore()
    for has, other in sides:

        @pl.when(has)
        def _():
            pl.semaphore_signal(sem, inc=1, device_id=(shot, other), device_id_type=MESH)

    pl.semaphore_wait(sem, has_up.astype(jnp.int32) + has_dn.astype(jnp.int32))

    def halo(slot, side, c):
        return pltpu.make_async_remote_copy(
            src_ref=hs.at[slot, side, c],
            dst_ref=hr.at[slot, 1 - side, c],
            send_sem=ssem.at[slot, side, c],
            recv_sem=rsem.at[slot, 1 - side, c],
            device_id=(shot, sides[side][1]),
            device_id_type=MESH,
        )

    def halo_in(slot, side, c):
        return pltpu.make_async_remote_copy(
            src_ref=hs.at[slot, side, c],
            dst_ref=hr.at[slot, side, c],
            send_sem=ssem.at[slot, side, c],
            recv_sem=rsem.at[slot, side, c],
            device_id=(shot, sides[side][1]),
            device_id_type=MESH,
        )

    zeros8 = jnp.zeros((32, 8, 128), F32)
    for par in range(2):
        U[par, :, 0:8, :] = zeros8
        U[par, :, 40:48, :] = zeros8
        for buf in (H, LO):
            buf[par, 0:32, :] = jnp.zeros((32, LANES), BF16)
            buf[par, 544:576, :] = jnp.zeros((32, LANES), BF16)
    for c in range(4):
        for k in range(8):
            cb = 8 * c + k
            value = u_in[0, :, cb * 128 : (cb + 1) * 128]
            U[0, cb, 8:40, :] = value
            hs[0, 0, c, k] = value[0:4]
            hs[0, 1, c, k] = value[28:32]
            U[1, cb, 8:40, :] = w_in[0, :, cb * 128 : (cb + 1) * 128]
        for side in range(2):

            @pl.when(sides[side][0])
            def _():
                halo(0, side, c).start()

    for j in range(16):
        hi, lo = split2(u_in[0, :, j * LANES : (j + 1) * LANES])
        H[0, 32 + 32 * j : 64 + 32 * j, :] = hi
        LO[0, 32 + 32 * j : 64 + 32 * j, :] = lo
    G[...] = jnp.zeros(G.shape, F32)

    receivers = rec[...]
    column = receivers & (PLANE - 1)
    level = (receivers >> 12) - sub * ROWS
    depth_at = lax.broadcasted_iota(jnp.int32, (ROWS, LANES), 0)
    at_depth = depth_at == level
    for t in range(STEPS):
        value = jnp.where(at_depth, tr[0, t : t + 1, :], 0.0)
        for s, v in enumerate(split3(value)):
            T3[s, 32 * t : 32 * t + 32, 0:LANES] = v
    cell = lax.broadcasted_iota(jnp.int32, (LANES, LANES), 0)

    def source_block(j, carry):
        onehot = (cell + j * LANES == column).astype(F32).astype(BF16)
        total = dot(T3[0, :, 0:LANES], onehot, True)
        total = total + dot(T3[1, :, 0:LANES], onehot, True)
        total = total + dot(T3[2, :, 0:LANES], onehot, True)
        for t in range(STEPS):
            S[t, j] = total[32 * t : 32 * t + 32]
        return carry

    lax.fori_loop(0, 16, source_block, 0)

    src = lax.broadcasted_iota(jnp.int32, (512, 512), 0)
    dst = lax.broadcasted_iota(jnp.int32, (512, 512), 1)
    moved = ((src >> 4) & 7) * 64 + (src >> 7) * 16 + (src & 15)
    PM[...] = (moved == dst).astype(F32).astype(BF16)

    for a in range(4):
        for h in range(2):
            row = 32 * (2 * a + h)
            wide = jnp.concatenate(
                [qt[4 * a + b, :, 128 * h : 128 * h + 128] for b in range(4)], axis=1
            )
            for s, v in enumerate(split3(wide * C1)):
                T3[s, row : row + 32, :] = v
    for n in range(2):
        perm = PM[:, LANES * n : LANES * n + LANES]
        total = dot(T3[0], perm) + dot(T3[1], perm) + dot(T3[2], perm)
        for k in range(8):
            Q[2 * k + n] = total[32 * k : 32 * k + 32]

    def one_step(t, carry):
        par = lax.rem(t, 2)
        nxt = 1 - par
        for c in range(4):
            for side in range(2):

                @pl.when(sides[side][0])
                def _():
                    halo(par, side, c).wait_send()
                    halo_in(par, side, c).wait_recv()
                    first = 4 if side == 0 else 40
                    for k in range(8):
                        U[par, 8 * c + k, first : first + 4, :] = hr[par, side, c, k]

            lateral = None
            for d in range(3):
                rows = pl.ds(128 * c + 32 * d, 128)
                for buf in (H, LO):
                    term = dot(buf[par, rows, :], mats[d])
                    lateral = term if lateral is None else lateral + term
            for jj in range(4):
                j = 4 * c + jj
                half = []
                for h in range(2):
                    cb = 2 * j + h
                    here = U[par, cb, 8:40, :]
                    acc = (3.0 * REL[0]) * here
                    for reach in range(1, 5):
                        beside = U[par, cb, 8 + reach : 40 + reach, :] + U[par, cb, 8 - reach : 40 - reach, :]
                        acc = acc + (beside if reach == 1 else REL[reach] * beside)
                    lanes = slice(128 * h, 128 * h + 128)
                    acc = acc + lateral[32 * jj : 32 * jj + 32, lanes]
                    new = 2.0 * here - U[nxt, cb, 8:40, :] + Q[j, :, lanes] * acc + S[t, j, :, lanes]
                    G[j, :, lanes] += fwd[0, t, :, cb * 128 : cb * 128 + 128].astype(F32) * new
                    U[nxt, cb, 8:40, :] = new
                    hs[nxt, 0, c, 2 * jj + h] = new[0:4]
                    hs[nxt, 1, c, 2 * jj + h] = new[28:32]
                    half.append(new)
                hi, lo = split2(jnp.concatenate(half, axis=1))
                H[nxt, 32 + 32 * j : 64 + 32 * j, :] = hi
                LO[nxt, 32 + 32 * j : 64 + 32 * j, :] = lo
            for side in range(2):

                @pl.when(sides[side][0] & (t < STEPS - 1))
                def _():
                    halo(nxt, side, c).start()

        return carry

    lax.fori_loop(0, STEPS, one_step, 0)

    for cb in range(32):
        fin_out[0, :, cb * 128 : (cb + 1) * 128] = U[STEPS % 2, cb, 8:40, :].astype(BF16)
    for k in range(8):
        wide = jnp.concatenate([G[2 * k], G[2 * k + 1]], axis=1)
        for s, v in enumerate(split3(wide)):
            T3[s, 32 * k : 32 * k + 32, :] = v
    for n in range(2):
        perm = PM[LANES * n : LANES * n + LANES, :]
        total = dot(T3[0], perm, True) + dot(T3[1], perm, True) + dot(T3[2], perm, True)
        for k in range(8):
            a, h = k // 2, k % 2
            for b in range(2):
                gt_out[4 * a + 2 * n + b, :, 128 * h : 128 * h + 128] = total[
                    32 * k : 32 * k + 32, 128 * b : 128 * b + 128
                ]


def time_steps(rec_index, traces, adj_now, adj_prev, fwd_lap, tiles):
    vmem = pl.BlockSpec(memory_space=pltpu.VMEM)
    mats = jnp.asarray(lateral_matrices(), BF16)
    scratch = [
        pltpu.VMEM((2, 32, 48, 128), F32),
        pltpu.VMEM((2, 576, LANES), BF16),
        pltpu.VMEM((2, 576, LANES), BF16),
        pltpu.VMEM((16, ROWS, LANES), F32),
        pltpu.VMEM((16, ROWS, LANES), F32),
        pltpu.VMEM((STEPS, 16, ROWS, LANES), F32),
        pltpu.VMEM((512, 512), BF16),
        pltpu.VMEM((3, 256, 512), BF16),
        pltpu.VMEM((2, 2, 4, 8, 4, 128), F32),
        pltpu.VMEM((2, 2, 4, 8, 4, 128), F32),
        pltpu.SemaphoreType.DMA((2, 2, 4)),
        pltpu.SemaphoreType.DMA((2, 2, 4)),
    ]
    return pl.pallas_call(
        steps_kernel,
        out_shape=(
            jax.ShapeDtypeStruct((16, ROWS, LANES), F32),
            jax.ShapeDtypeStruct((1, ROWS, PLANE), BF16),
        ),
        in_specs=[vmem] * 7,
        out_specs=(vmem, vmem),
        scratch_shapes=scratch,
        compiler_params=pltpu.CompilerParams(
            collective_id=1, has_side_effects=True, vmem_limit_bytes=VMEM_LIMIT
        ),
    )(rec_index, traces, adj_now, adj_prev, fwd_lap, tiles, mats)


def scatter_kernel(ts, tl, g16, out_ref, *scratch):
    gg = scratch[:NCH]
    rel_s = scratch[NCH : 2 * NCH]
    rel_r = scratch[2 * NCH : 3 * NCH]
    blk_s = scratch[3 * NCH : 4 * NCH]
    blk_r = scratch[4 * NCH : 5 * NCH]
    col = scratch[5 * NCH : 6 * NCH]
    zrel_r = scratch[6 * NCH : 7 * NCH]
    zblk_s = scratch[7 * NCH : 8 * NCH]
    zblk_r = scratch[8 * NCH : 9 * NCH]
    tabv, tab, ssem, rsem, lsem = scratch[9 * NCH :]
    links = Links()
    here = {"y": links.y, "x": links.x, "z": links.z}
    z = links.z
    links.barrier()
    sent = []

    def go(copy):
        copy.start()
        sent.append(copy)
        return copy

    a1, a2 = {}, {}
    for c in range(NCH):
        first = axes_of(c)[1]
        m = here[first]
        for d, delta in enumerate((1, -1)):
            a1[c, d] = go(
                rcopy(
                    links, first, delta, g16.at[:, pl.ds(c * R, R)],
                    gg[c].at[pl.ds(m * 16, 16)], ssem, rsem, c, d,
                )
            )

    row_at = lax.broadcasted_iota(jnp.int32, (8, 128), 0)
    lane_at = lax.broadcasted_iota(jnp.int32, (8, 128), 1)

    def table_row(p, acc):
        for order in range(2):
            first = ("y", "x")[order]
            m = here[first]
            for src in range(4):
                slot = ts[tl[links.step(first, src - m), p]]
                owner, at = slot_parts(slot, order)
                at = jnp.where(owner == m, at, -1)
                hit = (row_at == order * 4 + src) & (lane_at == at)
                acc = jnp.where(hit, src * 16 + p, acc)
        return acc

    tabv[...] = lax.fori_loop(0, 16, table_row, jnp.full((8, 128), 64, jnp.int32))
    fill = pltpu.make_async_copy(tabv, tab, lsem)
    fill.start()
    for c in range(NCH):
        m = here[axes_of(c)[1]]
        gg[c][64] = jnp.zeros((R, LANES), F32)
        for p in range(16):
            gg[c][m * 16 + p] = g16[p, c * R : (c + 1) * R, :]
    fill.wait()

    for c in range(NCH):
        first = axes_of(c)[1]
        m = here[first]
        for d, delta in enumerate((1, -1)):
            a1[c, d].wait_recv()
            piece = gg[c].at[pl.ds(ring(m - delta) * 16 + 8 * d, 8)]
            a2[c, d] = go(rcopy(links, first, delta, piece, piece, ssem, rsem, c, 2 + d))

    def partial(c, line, e):
        order = c % 2
        total = None
        for src in range(4):
            term = gg[c][tab[order * 4 + src, line * 16 + e]]
            total = term if total is None else total + term
        return total

    rl, bl = {}, {}
    for c in range(NCH):
        axis = axes_of(c)[0]
        line = here[axis]
        for d in range(2):
            a2[c, d].wait_recv()
        for d, delta in enumerate((1, -1)):
            for e in range(8):
                rel_s[c][d, e] = partial(c, ring(line + 2), 8 * d + e)
            rl[c, d] = go(
                rcopy(links, axis, delta, rel_s[c].at[d], rel_r[c].at[d], ssem, rsem, c, 4 + d)
            )
    for c in range(NCH):
        axis = axes_of(c)[0]
        line = here[axis]
        for d, delta in enumerate((1, -1)):
            rl[c, d].wait_recv()
            for e in range(16):
                value = partial(c, ring(line + delta), e)
                if e // 8 == d:
                    value = value + rel_r[c][d, e % 8]
                blk_s[c][d, e] = value
            bl[c, d] = go(
                rcopy(links, axis, delta, blk_s[c].at[d], blk_r[c].at[d], ssem, rsem, c, 6 + d)
            )
    zr, zb = {}, {}
    for c in range(NCH):
        line = here[axes_of(c)[0]]
        for e in range(16):
            col[c][e] = partial(c, line, e)
        for d in range(2):
            bl[c, d].wait_recv()
        for e in range(16):
            col[c][e] += blk_r[c][0, e] + blk_r[c][1, e]
        for d, delta in enumerate((1, -1)):
            zr[c, d] = go(
                rcopy(
                    links, "z", delta, col[c].at[pl.ds(ring(z + 2) * 4 + 2 * d, 2)],
                    zrel_r[c].at[d], ssem, rsem, c, 8 + d,
                )
            )
    for c in range(NCH):
        for d, delta in enumerate((1, -1)):
            zr[c, d].wait_recv()
            for t in range(4):
                value = col[c][ring(z + delta) * 4 + t]
                if t // 2 == d:
                    value = value + zrel_r[c][d, t % 2]
                zblk_s[c][d, t] = value
            zb[c, d] = go(
                rcopy(links, "z", delta, zblk_s[c].at[d], zblk_r[c].at[d], ssem, rsem, c, 10 + d)
            )
    for c in range(NCH):
        for d in range(2):
            zb[c, d].wait_recv()
        for t in range(4):
            out_ref[t, c * R : (c + 1) * R, :] = col[c][z * 4 + t] + zblk_r[c][0, t] + zblk_r[c][1, t]
    for copy in sent:
        copy.wait_send()


def scatter_tiles(tile_slot, tile_list, grad):
    smem = pl.BlockSpec(memory_space=pltpu.SMEM)
    vmem = pl.BlockSpec(memory_space=pltpu.VMEM)
    scratch = (
        [pltpu.VMEM((65, R, LANES), F32)] * NCH
        + [pltpu.VMEM((2, 8, R, LANES), F32)] * (2 * NCH)
        + [pltpu.VMEM((2, 16, R, LANES), F32)] * (2 * NCH)
        + [pltpu.VMEM((16, R, LANES), F32)] * NCH
        + [pltpu.VMEM((2, 2, R, LANES), F32)] * NCH
        + [pltpu.VMEM((2, 4, R, LANES), F32)] * (2 * NCH)
        + [pltpu.VMEM((8, 128), jnp.int32), pltpu.SMEM((8, 128), jnp.int32)]
        + [pltpu.SemaphoreType.DMA((NCH, 12))] * 2
        + [pltpu.SemaphoreType.DMA]
    )
    return pl.pallas_call(
        scatter_kernel,
        out_shape=jax.ShapeDtypeStruct((4, ROWS, LANES), F32),
        in_specs=[smem, smem, vmem],
        out_specs=vmem,
        scratch_shapes=scratch,
        compiler_params=pltpu.CompilerParams(
            collective_id=2, has_side_effects=True, vmem_limit_bytes=VMEM_LIMIT
        ),
    )(tile_slot, tile_list, grad)


def body(q_model, tile_slot, tile_list, rec_index, traces, adj_now, adj_prev, fwd_lap):
    tiles = gather_tiles(tile_slot, tile_list, q_model)
    grad, final = time_steps(rec_index, traces, adj_now, adj_prev, fwd_lap, tiles)
    return scatter_tiles(tile_slot, tile_list, grad), final


def solution(mesh):
    in_specs = (
        P("shot", "sub", None),
        P(),
        P(),
        P("shot", None),
        P("shot", None, None),
        P("shot", "sub", None),
        P("shot", "sub", None),
        P("shot", None, "sub", None),
    )
    out_specs = (P("shot", "sub", None), P("shot", "sub", None))
    return jax.shard_map(body, mesh=mesh, in_specs=in_specs, out_specs=out_specs, check_vma=False)
```

time: 739 us -> 122 us (0.17); the launches traced: 728 us -> 122 us
  other arithmetic: 272 us -> 0 us
  local copies, waits for them, and re-layouts: 194 us -> 4.63 us
  waiting for transfers between devices: 177 us -> 0 us
  Pallas kernels: 0 us -> 117 us
  starting transfers between devices: 64 us -> 0 us
  between operations: 15.2 us -> 0.65 us
    add x8 -> x0, other arithmetic: 180 us -> none  [the longest x7 171 us: body(): 2.0 * current - previous + speed * laplace(current, width_y) + source]
    pallas_call x0 -> x3, Pallas kernels: none -> 117 us  [the longest x1 43.4 us: gather_tiles(): pl.pallas_call(gather_kernel, out_shape=jax.ShapeDtypeStruct((16, ROWS, L...]
    all_to_all x1 -> x0, waiting for transfers between devices: 97.8 us -> none  [body(): lax.all_to_all(outgoing_grad, 'shot', split_axis=0, concat_axis=0, tiled=...]
    all_gather x1 -> x0, waiting for transfers between devices: 79 us -> none  [body(): piece = lax.all_gather(flat_model, 'shot', axis=0, tiled=True)]
    slice x24 -> x0, local copies, waits for them, and re-layouts: 56.8 us -> none  [the longest x15 35.5 us: with_halo(): lax.slice_in_dim(cells, cells.shape[dim] - width, cells.shape[dim], axis=...]
    ppermute x16 -> x0, starting transfers between devices: 53.7 us -> none  [the longest x8 27 us: with_halo(): lax.ppermute(head, axis, [((i + 1) % count, i) for i in range(ends)])]
    ppermute x16 -> x0, local copies, waits for them, and re-layouts: 38.7 us -> none  [the longest x8 19.4 us: with_halo(): lax.ppermute(tail, axis, [(i, (i + 1) % count) for i in range(ends)])]
    unnamed x128 -> x3, local copies, waits for them, and re-layouts: 38.2 us -> 4.63 us
  transfers between devices with their start and end apart: 18 -> 0, of which waited for: 2 -> 0; matrix products, arithmetic and copies ran while one was open for 15% -> 0% of each run, Pallas kernels for 0% -> 0%
where the time goes in v1:
time: 122 us
  Pallas kernels  117 us (96%)
  local copies, waits for them, and re-layouts  4.63 us (4%)
    pallas_call x1, Pallas kernels, gather_tiles(): pl.pallas_call(gather_kernel, out_shape=jax.ShapeDtypeStruct((16, ROWS, L...  43.4 us
    pallas_call x1, Pallas kernels, scatter_tiles(): pl.pallas_call(scatter_kernel, out_shape=jax.ShapeDtypeStruct((4, ROWS, L...  38.4 us
    pallas_call x1, Pallas kernels, time_steps(): pl.pallas_call(steps_kernel, out_shape=(jax.ShapeDtypeStruct((16, ROWS, L...  34.8 us
    unnamed x3, local copies, waits for them, and re-layouts  4.63 us

profile of v1, /device:TPU:1, one launch (start us, length us, event | category | flops | bytes accessed | tf_op | source)
XLA Modules:
  0.0 122.0 jit_solution(5747232494462123700)
XLA Ops:
  0.6 1.4 %copy.12.tl = s32[64,16]{1,0:T(8,128)} copy(s32[64,16]{0,1:T(8,128)} %param.11) | data formatting | bytes 8192 | tf_op args[2]
  2.0 43.4 %shard_map.104.qt = f32[16,32,256]{2,1,0:T(8,128)} custom-call(s32[256]{0:T(256)} %ts.3, s32[64,16]{1,0:T(8,128)} %copy.12.tl, f32[4,32,256]{2,1,0:T(8,128)} %q_ref.1), custom_call_target="tpu_custom_call" | custom-call | tf_op jit(solution)/shard_map/pallas_call | solution.py:214
  45.5 34.8 %shard_map.105 = (f32[16,32,256]{2,1,0:T(8,128)}, bf16[1,32,4096]{2,1,0:T(8,128)(2,1)}) custom-call(s32[1,256]{1,0:T(1,128)} %rec.1, f32[1,8,256]{2,1,0:T(8,128)} %tr.1, f32[1,32,4096]{2,1,0:T(8,128)} %u_in.1, f32[1,32,4096]{2,1,0:T(8,128)} %w_in.1, bf16[1,8,32,4096]{3,2,1,0:T(8,128)(2,1)} %fwd.1, f32[16,32,256]{2,1,0:T(8,128)} %shard_map.104.qt, ...), custom_call_target="tpu_custom_call" | custom-call | tf_op jit(solution)/shard_map/pallas_call | solution.py:432
  80.3 38.4 %shard_map.106 = f32[4,32,256]{2,1,0:T(8,128)} custom-call(s32[256]{0:T(256)} %ts.3, s32[64,16]{1,0:T(8,128)} %copy.12.tl, f32[16,32,256]{2,1,0:T(8,128)} %get-tuple-element.4.g16), custom_call_target="tpu_custom_call" | custom-call | tf_op jit(solution)/shard_map/pallas_call | solution.py:597
  118.7 1.6 %copy.15 = f32[4,32,256]{2,1,0:T(8,128)} copy(f32[4,32,256]{2,1,0:T(8,128)} %shard_map.106) | data formatting | bytes 262144
  120.3 1.7 %copy.16 = bf16[1,32,4096]{2,1,0:T(8,128)(2,1)} copy(bf16[1,32,4096]{2,1,0:T(8,128)(2,1)} %get-tuple-element.9) | data formatting | bytes 524288

commit v2 on v0

v2 whole, which is shorter than its diff:
```python
import jax
import jax.numpy as jnp
import numpy as np
from jax import lax
from jax.experimental import pallas as pl
from jax.experimental.pallas import tpu as pltpu
from jax.sharding import PartitionSpec as P

TS = 16
STEPS = 8
ROWS = 32
LANES = 256
PLANE = 4096
COEFFS = (-205.0 / 72.0, 8.0 / 5.0, -1.0 / 5.0, 8.0 / 315.0, -1.0 / 560.0)
C1 = COEFFS[1]
REL = tuple(c / C1 for c in COEFFS)

NCH = 4
R = ROWS // NCH
HC = 8
CB = 32 // HC

MESH = pl.DeviceIdType.MESH
VMEM_LIMIT = 60 * 1024 * 1024
F32 = jnp.float32
BF16 = jnp.bfloat16
DIRS = ((0, 1), (1, -1))


def lateral_matrices():
    out = np.zeros((3, LANES, LANES), np.float32)
    k = np.arange(LANES)[:, None]
    n = np.arange(LANES)[None, :]
    for d in (-1, 0, 1):
        dx = 4 * d + k // 64 - n // 64
        dy = k % 64 - n % 64
        for reach in range(1, 5):
            hit = ((dx == 0) & (np.abs(dy) == reach)) | ((dy == 0) & (np.abs(dx) == reach))
            out[d + 1][hit] = REL[reach]
    return np.concatenate([out, out]).reshape(6 * LANES, LANES)


def shot_at(y, x, z):
    return (y * 4 + x) * 4 + z


def ring(v):
    return (v + 8) % 4


class Links:
    def __init__(self):
        me = lax.axis_index("shot")
        self.at = {"y": me // 16, "x": (me // 4) % 4, "z": me % 4}
        self.shot = me
        self.sub = lax.axis_index("sub")

    def step(self, axis, delta):
        at = dict(self.at)
        at[axis] = ring(at[axis] + delta)
        return shot_at(at["y"], at["x"], at["z"])

    def copy(self, axis, delta, src, dst, sems, c, k):
        return pltpu.make_async_remote_copy(
            src_ref=src,
            dst_ref=dst,
            send_sem=sems[0].at[c, k],
            recv_sem=sems[1].at[c, k],
            device_id=(self.step(axis, delta), self.sub),
            device_id_type=MESH,
        )


def axes_of(c):
    return ("x", "y") if c % 2 == 0 else ("y", "x")


def slot_parts(slot, order):
    if order == 0:
        return slot // 64, slot % 64
    return (slot // 16) % 4, (slot // 64) * 16 + slot % 16


class Gather:
    def __init__(self, links, ts, tl, q_ref, QF, g, rel_s, rel_r, blk_s, blk_r, sems):
        self.links, self.ts, self.tl, self.q_ref, self.QF = links, ts, tl, q_ref, QF
        self.g, self.rel_s, self.rel_r, self.blk_s, self.blk_r = g, rel_s, rel_r, blk_s, blk_r
        self.sems = sems
        self.sent = []
        self.live = {}

    def go(self, name, c, d, axis, delta, src, dst, k):
        copy = self.links.copy(axis, delta, src, dst, self.sems, c, k + d)
        copy.start()
        self.sent.append(copy)
        self.live[name, c, d] = copy

    def got(self, name, c, d):
        self.live[name, c, d].wait_recv()

    def line(self, c):
        return self.links.at[axes_of(c)[0]]

    def part(self, c, line, zz, t0=0, n=4):
        return self.g[c].at[pl.ds(line * 16 + zz * 4 + t0, n)]

    def start(self, c):
        z, line = self.links.at["z"], self.line(c)
        src = self.q_ref.at[:, pl.ds(c * R, R)]
        for d, delta in DIRS:
            self.go("zp1", c, d, "z", delta, src, self.part(c, line, z), 0)
        for d, delta in DIRS:
            self.go("a1own", c, d, axes_of(c)[0], delta, src, self.part(c, line, z), 4)

    def keep(self, c):
        z, line = self.links.at["z"], self.line(c)
        for t in range(4):
            self.g[c][line * 16 + z * 4 + t] = self.q_ref[t, c * R : (c + 1) * R, :]

    def zp2(self, c):
        z, line = self.links.at["z"], self.line(c)
        for d, delta in DIRS:
            self.got("zp1", c, d)
            piece = self.part(c, line, ring(z - delta), 2 * d, 2)
            self.go("zp2", c, d, "z", delta, piece, piece, 2)

    def spread(self, name, c, zz, k):
        piece = self.part(c, self.line(c), zz)
        for d, delta in DIRS:
            self.go(name, c, d, axes_of(c)[0], delta, piece, piece, k)

    def a1n(self, c):
        z = self.links.at["z"]
        self.spread("a1m", c, ring(z - 1), 6)
        self.spread("a1p", c, ring(z + 1), 8)

    def a1f(self, c):
        for d in range(2):
            self.got("zp2", c, d)
        self.spread("a1f", c, ring(self.links.at["z"] + 2), 10)

    def forward(self, come, name, c, zz, k):
        for d, delta in DIRS:
            self.got(come, c, d)
            piece = self.part(c, ring(self.line(c) - delta), zz, 2 * d, 2)
            self.go(name, c, d, axes_of(c)[0], delta, piece, piece, k)

    def a2own(self, c):
        self.forward("a1own", "a2own", c, self.links.at["z"], 12)

    def a2n(self, c):
        z = self.links.at["z"]
        self.forward("a1m", "a2m", c, ring(z - 1), 14)
        self.forward("a1p", "a2p", c, ring(z + 1), 16)

    def a2f(self, c):
        self.forward("a1f", "a2f", c, ring(self.links.at["z"] + 2), 18)

    def target(self, c, delta, p):
        slot = self.ts[self.tl[self.links.step(axes_of(c)[1], delta), p]]
        return slot_parts(slot, c % 2)

    def rel(self, c):
        last = axes_of(c)[1]
        for d in range(2):
            for name in ("a2own", "a2m", "a2p", "a2f"):
                self.got(name, c, d)
        for d, delta in DIRS:
            for p in range(8):
                _, at = self.target(c, 2, 8 * d + p)
                self.rel_s[c][d, p] = self.g[c][at]
            self.go("rel", c, d, last, delta, self.rel_s[c].at[d], self.rel_r[c].at[d], 20)

    def blk(self, c):
        last = axes_of(c)[1]
        mine = self.links.at[last]
        for d, delta in DIRS:
            self.got("rel", c, d)
            for p in range(16):
                owner, at = self.target(c, delta, p)
                value = self.g[c][at]
                if p // 8 == d:
                    value = jnp.where(owner == mine, value, self.rel_r[c][d, p % 8])
                self.blk_s[c][d, p] = value
            self.go("blk", c, d, last, delta, self.blk_s[c].at[d], self.blk_r[c].at[d], 22)

    def finish(self, c):
        mine = self.links.at[axes_of(c)[1]]
        blk_r = self.blk_r[c]
        for d in range(2):
            self.got("blk", c, d)
        for p in range(16):
            owner, at = self.target(c, 0, p)
            gap = ring(owner - mine)
            if p < 8:
                other = jnp.where(gap == 1, blk_r[1, p], blk_r[0, p])
            else:
                other = jnp.where(gap == 3, blk_r[0, p], blk_r[1, p])
            value = C1 * jnp.where(gap == 0, self.g[c][at], other)
            a, b = p // 4, p % 4
            for h in range(2):
                row = 32 * (2 * a + h) + c * R
                self.QF[row : row + R, 128 * b : 128 * b + 128] = value[:, 128 * h : 128 * h + 128]

    def drain(self):
        for copy in self.sent:
            copy.wait_send()


class Scatter:
    def __init__(
        self, links, tab, out_ref, gg, rel_s, rel_r, blk_s, blk_r, col, zrel_r, zblk_s, zblk_r, sems
    ):
        self.links, self.tab, self.out_ref, self.gg, self.col = links, tab, out_ref, gg, col
        self.rel_s, self.rel_r, self.blk_s, self.blk_r = rel_s, rel_r, blk_s, blk_r
        self.zrel_r, self.zblk_s, self.zblk_r = zrel_r, zblk_s, zblk_r
        self.sems = sems
        self.sent = []
        self.live = {}

    go = Gather.go
    got = Gather.got
    line = Gather.line
    drain = Gather.drain

    def first(self, c):
        return self.links.at[axes_of(c)[1]]

    def a1(self, c, half):
        for d, delta in DIRS:
            side = d if half == 0 else 1 - d
            piece = self.gg[c].at[pl.ds(self.first(c) * 16 + 8 * side, 8)]
            self.go(("a1", half), c, d, axes_of(c)[1], delta, piece, piece, 2 * half)

    def a2(self, c):
        for d, delta in DIRS:
            self.got(("a1", 0), c, d)
            piece = self.gg[c].at[pl.ds(ring(self.first(c) - delta) * 16 + 8 * d, 8)]
            self.go("a2", c, d, axes_of(c)[1], delta, piece, piece, 4)

    def partial(self, c, line, e):
        total = None
        for src in range(4):
            term = self.gg[c][self.tab[(c % 2) * 4 + src, line * 16 + e]]
            total = term if total is None else total + term
        return total

    def rel(self, c):
        for d in range(2):
            self.got(("a1", 1), c, d)
            self.got("a2", c, d)
        for d, delta in DIRS:
            for e in range(8):
                self.rel_s[c][d, e] = self.partial(c, ring(self.line(c) + 2), 8 * d + e)
            self.go(
                "rel", c, d, axes_of(c)[0], delta, self.rel_s[c].at[d], self.rel_r[c].at[d], 6
            )

    def own(self, c):
        for e in range(16):
            self.col[c][e] = self.partial(c, self.line(c), e)

    def blk(self, c):
        for d, delta in DIRS:
            self.got("rel", c, d)
            for e in range(16):
                value = self.partial(c, ring(self.line(c) + delta), e)
                if e // 8 == d:
                    value = value + self.rel_r[c][d, e % 8]
                self.blk_s[c][d, e] = value
            self.go(
                "blk", c, d, axes_of(c)[0], delta, self.blk_s[c].at[d], self.blk_r[c].at[d], 8
            )

    def zrel(self, c):
        z = self.links.at["z"]
        for d in range(2):
            self.got("blk", c, d)
        for e in range(16):
            self.col[c][e] += self.blk_r[c][0, e] + self.blk_r[c][1, e]
        for d, delta in DIRS:
            piece = self.col[c].at[pl.ds(ring(z + 2) * 4 + 2 * d, 2)]
            self.go("zrel", c, d, "z", delta, piece, self.zrel_r[c].at[d], 10)

    def zblk(self, c):
        z = self.links.at["z"]
        for d, delta in DIRS:
            self.got("zrel", c, d)
            for t in range(4):
                value = self.col[c][ring(z + delta) * 4 + t]
                if t // 2 == d:
                    value = value + self.zrel_r[c][d, t % 2]
                self.zblk_s[c][d, t] = value
            self.go("zblk", c, d, "z", delta, self.zblk_s[c].at[d], self.zblk_r[c].at[d], 12)

    def finish(self, c):
        z = self.links.at["z"]
        for d in range(2):
            self.got("zblk", c, d)
        for t in range(4):
            self.out_ref[t, c * R : (c + 1) * R, :] = (
                self.col[c][z * 4 + t] + self.zblk_r[c][0, t] + self.zblk_r[c][1, t]
            )


def split2(v):
    hi = v.astype(BF16)
    return hi, (v - hi.astype(F32)).astype(BF16)


def split3(v):
    hi = v.astype(BF16)
    rest = v - hi.astype(F32)
    mid = rest.astype(BF16)
    return hi, mid, (rest - mid.astype(F32)).astype(BF16)


def dot(a, b, transposed=False):
    dims = (((1,), (1,)), ((), ())) if transposed else (((1,), (0,)), ((), ()))
    return lax.dot_general(a, b, dims, preferred_element_type=F32)


def kernel(ts, tl, q_ref, rec, tr, u_in, w_in, fwd, mats, grad_out, fin_out, *scratch):
    scratch = list(scratch)

    def take(n):
        out = scratch[:n]
        del scratch[:n]
        return out

    U, H, LO, ACC, Q, G, S, PM, QF, T3, FW, hs, hr, tabv, tab = take(15)
    g, rel_s, rel_r, blk_s, blk_r = (take(NCH) for _ in range(5))
    gg, grel_s, grel_r, gblk_s, gblk_r = (take(NCH) for _ in range(5))
    col, zrel_r, zblk_s, zblk_r = (take(NCH) for _ in range(4))
    ssem, rsem, qs, qr, gs, gr, lsem = take(7)

    links = Links()
    shot, sub = links.shot, links.sub
    has_up, has_dn = sub > 0, sub < 3
    sides = ((has_up, sub - 1), (has_dn, sub + 1))
    load = pltpu.make_async_copy(fwd.at[0], FW, lsem.at[0])
    load.start()

    sem = pltpu.get_barrier_semaphore()
    for axis in ("y", "x", "z"):
        for delta in (1, -1):
            pl.semaphore_signal(
                sem, inc=1, device_id=(links.step(axis, delta), sub), device_id_type=MESH
            )
    for has, other in sides:

        @pl.when(has)
        def _():
            pl.semaphore_signal(sem, inc=1, device_id=(shot, other), device_id_type=MESH)

    pl.semaphore_wait(sem, 6 + has_up.astype(jnp.int32) + has_dn.astype(jnp.int32))

    def halo(slot, side, c):
        return pltpu.make_async_remote_copy(
            src_ref=hs.at[slot, side, c],
            dst_ref=hr.at[slot, 1 - side, c],
            send_sem=ssem.at[slot, side, c],
            recv_sem=rsem.at[slot, 1 - side, c],
            device_id=(shot, sides[side][1]),
            device_id_type=MESH,
        )

    def halo_in(slot, side, c):
        return pltpu.make_async_remote_copy(
            src_ref=hs.at[slot, side, c],
            dst_ref=hr.at[slot, side, c],
            send_sem=ssem.at[slot, side, c],
            recv_sem=rsem.at[slot, side, c],
            device_id=(shot, sides[side][1]),
            device_id_type=MESH,
        )

    def init_fields():
        zeros8 = jnp.zeros((32, 8, 128), F32)
        for par in range(2):
            U[par, :, 0:8, :] = zeros8
            U[par, :, 40:48, :] = zeros8
        for buf in (H, LO):
            buf[0:32, :] = jnp.zeros((32, LANES), BF16)
            buf[544:576, :] = jnp.zeros((32, LANES), BF16)
        for c in range(HC):
            for k in range(CB):
                cb = CB * c + k
                value = u_in[0, :, cb * 128 : (cb + 1) * 128]
                U[0, cb, 8:40, :] = value
                hs[0, 0, c, k] = value[0:4]
                hs[0, 1, c, k] = value[28:32]
                U[1, cb, 8:40, :] = w_in[0, :, cb * 128 : (cb + 1) * 128]
            for side in range(2):

                @pl.when(sides[side][0])
                def _():
                    halo(0, side, c).start()

        for j in range(16):
            hi, lo = split2(u_in[0, :, j * LANES : (j + 1) * LANES])
            H[32 + 32 * j : 64 + 32 * j, :] = hi
            LO[32 + 32 * j : 64 + 32 * j, :] = lo
        G[...] = jnp.zeros(G.shape, F32)

    receivers = rec[...]
    column = receivers & (PLANE - 1)
    level = (receivers >> 12) - sub * ROWS

    def source_values():
        depth_at = lax.broadcasted_iota(jnp.int32, (ROWS, LANES), 0)
        at_depth = depth_at == level
        for t in range(STEPS):
            value = jnp.where(at_depth, tr[0, t : t + 1, :], 0.0)
            for s, v in enumerate(split3(value)):
                T3[s, 32 * t : 32 * t + 32, 0:LANES] = v

    def source_block(j, carry):
        cell = lax.broadcasted_iota(jnp.int32, (LANES, LANES), 0)
        onehot = (cell + j * LANES == column).astype(F32).astype(BF16)
        total = dot(T3[0, :, 0:LANES], onehot, True)
        total = total + dot(T3[1, :, 0:LANES], onehot, True)
        total = total + dot(T3[2, :, 0:LANES], onehot, True)
        for t in range(STEPS):
            S[t, j] = total[32 * t : 32 * t + 32]
        return carry

    def sources(first, last):
        lax.fori_loop(first, last, source_block, 0)

    def permutation():
        src = lax.broadcasted_iota(jnp.int32, (512, 512), 0)
        dst = lax.broadcasted_iota(jnp.int32, (512, 512), 1)
        moved = ((src >> 4) & 7) * 64 + (src >> 7) * 16 + (src & 15)
        PM[...] = (moved == dst).astype(F32).astype(BF16)

    def table():
        row_at = lax.broadcasted_iota(jnp.int32, (8, 128), 0)
        lane_at = lax.broadcasted_iota(jnp.int32, (8, 128), 1)

        def table_row(p, acc):
            for order in range(2):
                first = ("y", "x")[order]
                m = links.at[first]
                for src in range(4):
                    slot = ts[tl[links.step(first, src - m), p]]
                    owner, at = slot_parts(slot, order)
                    at = jnp.where(owner == m, at, -1)
                    hit = (row_at == order * 4 + src) & (lane_at == at)
                    acc = jnp.where(hit, src * 16 + p, acc)
            return acc

        tabv[...] = lax.fori_loop(0, 16, table_row, jnp.full((8, 128), 64, jnp.int32))
        for c in range(NCH):
            gg[c][64] = jnp.zeros((R, LANES), F32)

    gather = Gather(links, ts, tl, q_ref, QF, g, rel_s, rel_r, blk_s, blk_r, (qs, qr))
    A, B = (0, 1), (2, 3)

    def each(step, chunks):
        for c in chunks:
            step(c)

    each(gather.start, A)
    each(gather.start, B)
    init_fields()
    each(gather.keep, A + B)
    each(gather.zp2, A)
    each(gather.a1n, A)
    each(gather.a2own, A)
    source_values()
    sources(0, 4)
    each(gather.zp2, B)
    each(gather.a1f, A)
    each(gather.a1n, B)
    each(gather.a2n, A)
    each(gather.a2own, B)
    sources(4, 8)
    each(gather.a2f, A)
    each(gather.a1f, B)
    each(gather.a2n, B)
    sources(8, 12)
    each(gather.rel, A)
    each(gather.a2f, B)
    sources(12, 16)
    each(gather.blk, A)
    permutation()
    each(gather.rel, B)
    table()
    fill = pltpu.make_async_copy(tabv, tab, lsem.at[1])
    fill.start()
    each(gather.finish, A)
    each(gather.blk, B)
    fill.wait()
    load.wait()
    each(gather.finish, B)
    gather.drain()

    for k in range(8):
        for s, v in enumerate(split3(QF[32 * k : 32 * k + 32, :])):
            T3[s, 32 * k : 32 * k + 32, :] = v
    for n in range(2):
        perm = PM[:, LANES * n : LANES * n + LANES]
        total = dot(T3[0], perm) + dot(T3[1], perm) + dot(T3[2], perm)
        for k in range(8):
            Q[2 * k + n] = total[32 * k : 32 * k + 32]

    def one_step(t, carry):
        par = lax.rem(t, 2)
        nxt = 1 - par
        wide = jnp.concatenate(
            [buf[32 * d : 32 * d + 512, :] for buf in (H, LO) for d in range(3)], axis=1
        )
        ACC[...] = dot(wide, mats[...])
        for c in range(HC):
            for side in range(2):

                @pl.when(sides[side][0])
                def _():
                    halo(par, side, c).wait_send()
                    halo_in(par, side, c).wait_recv()
                    first = 4 if side == 0 else 40
                    for k in range(CB):
                        U[par, CB * c + k, first : first + 4, :] = hr[par, side, c, k]

            for jj in range(CB // 2):
                j = CB // 2 * c + jj
                half = []
                for h in range(2):
                    cb = 2 * j + h
                    here = U[par, cb, 8:40, :]
                    lanes = slice(128 * h, 128 * h + 128)
                    acc = (3.0 * REL[0]) * here + ACC[32 * j : 32 * j + 32, lanes]
                    for reach in range(1, 5):
                        beside = U[par, cb, 8 + reach : 40 + reach, :] + U[par, cb, 8 - reach : 40 - reach, :]
                        acc = acc + (beside if reach == 1 else REL[reach] * beside)
                    new = 2.0 * here - U[nxt, cb, 8:40, :] + Q[j, :, lanes] * acc + S[t, j, :, lanes]
                    U[nxt, cb, 8:40, :] = new
                    hs[nxt, 0, c, 2 * jj + h] = new[0:4]
                    hs[nxt, 1, c, 2 * jj + h] = new[28:32]
                    G[j, :, lanes] += FW[t, :, cb * 128 : cb * 128 + 128].astype(F32) * new
                    half.append(new)
                hi, lo = split2(jnp.concatenate(half, axis=1))
                H[32 + 32 * j : 64 + 32 * j, :] = hi
                LO[32 + 32 * j : 64 + 32 * j, :] = lo
            for side in range(2):

                @pl.when(sides[side][0] & (t < STEPS - 1))
                def _():
                    halo(nxt, side, c).start()

        return carry

    lax.fori_loop(0, STEPS, one_step, 0)

    scatter = Scatter(
        links, tab, grad_out, gg, grel_s, grel_r, gblk_s, gblk_r, col, zrel_r, zblk_s, zblk_r, (gs, gr)
    )
    for k in range(8):
        wide = jnp.concatenate([G[2 * k], G[2 * k + 1]], axis=1)
        for s, v in enumerate(split3(wide)):
            T3[s, 32 * k : 32 * k + 32, :] = v
    for n in range(2):
        perm = PM[LANES * n : LANES * n + LANES, :]
        total = dot(T3[0], perm, True) + dot(T3[1], perm, True) + dot(T3[2], perm, True)
        for k in range(8):
            a, h = k // 2, k % 2
            for b in range(2):
                for c in range(NCH):
                    at = scatter.first(c) * 16 + 4 * a + 2 * n + b
                    row = 32 * k + c * R
                    gg[c][at, :, 128 * h : 128 * h + 128] = total[
                        row : row + R, 128 * b : 128 * b + 128
                    ]
    for c in A:
        scatter.a1(c, 0)
        scatter.a1(c, 1)
    for c in B:
        scatter.a1(c, 0)
    for cb in range(32):
        fin_out[0, :, cb * 128 : (cb + 1) * 128] = U[STEPS % 2, cb, 8:40, :].astype(BF16)
    each(scatter.a2, A)
    for c in B:
        scatter.a1(c, 1)
    each(scatter.a2, B)
    each(scatter.rel, A)
    each(scatter.own, A)
    each(scatter.blk, A)
    each(scatter.rel, B)
    each(scatter.own, B)
    each(scatter.zrel, A)
    each(scatter.blk, B)
    each(scatter.zblk, A)
    each(scatter.finish, A)
    each(scatter.zrel, B)
    each(scatter.zblk, B)
    each(scatter.finish, B)
    scatter.drain()


def body(q_model, tile_slot, tile_list, rec_index, traces, adj_now, adj_prev, fwd_lap):
    smem = pl.BlockSpec(memory_space=pltpu.SMEM)
    vmem = pl.BlockSpec(memory_space=pltpu.VMEM)
    mats = jnp.asarray(lateral_matrices(), BF16)
    scratch = [
        pltpu.VMEM((2, 32, 48, 128), F32),
        pltpu.VMEM((576, LANES), BF16),
        pltpu.VMEM((576, LANES), BF16),
        pltpu.VMEM((512, LANES), F32),
        pltpu.VMEM((16, ROWS, LANES), F32),
        pltpu.VMEM((16, ROWS, LANES), F32),
        pltpu.VMEM((STEPS, 16, ROWS, LANES), F32),
        pltpu.VMEM((512, 512), BF16),
        pltpu.VMEM((256, 512), F32),
        pltpu.VMEM((3, 256, 512), BF16),
        pltpu.VMEM((STEPS, ROWS, PLANE), BF16),
        pltpu.VMEM((2, 2, HC, CB, 4, 128), F32),
        pltpu.VMEM((2, 2, HC, CB, 4, 128), F32),
        pltpu.VMEM((8, 128), jnp.int32),
        pltpu.SMEM((8, 128), jnp.int32),
    ]
    scratch += [pltpu.VMEM((64, R, LANES), F32)] * NCH
    scratch += [pltpu.VMEM((2, 8, R, LANES), F32)] * (2 * NCH)
    scratch += [pltpu.VMEM((2, 16, R, LANES), F32)] * (2 * NCH)
    scratch += [pltpu.VMEM((65, R, LANES), F32)] * NCH
    scratch += [pltpu.VMEM((2, 8, R, LANES), F32)] * (2 * NCH)
    scratch += [pltpu.VMEM((2, 16, R, LANES), F32)] * (2 * NCH)
    scratch += [pltpu.VMEM((16, R, LANES), F32)] * NCH
    scratch += [pltpu.VMEM((2, 2, R, LANES), F32)] * NCH
    scratch += [pltpu.VMEM((2, 4, R, LANES), F32)] * (2 * NCH)
    scratch += [pltpu.SemaphoreType.DMA((2, 2, HC))] * 2
    scratch += [pltpu.SemaphoreType.DMA((NCH, 24))] * 2
    scratch += [pltpu.SemaphoreType.DMA((NCH, 14))] * 2
    scratch += [pltpu.SemaphoreType.DMA((2,))]
    return pl.pallas_call(
        kernel,
        out_shape=(
            jax.ShapeDtypeStruct((4, ROWS, LANES), F32),
            jax.ShapeDtypeStruct((1, ROWS, PLANE), BF16),
        ),
        in_specs=[smem, smem] + [vmem] * 5 + [pl.BlockSpec(memory_space=pl.ANY), vmem],
        out_specs=(vmem, vmem),
        scratch_shapes=scratch,
        compiler_params=pltpu.CompilerParams(
            collective_id=0, has_side_effects=True, vmem_limit_bytes=VMEM_LIMIT
        ),
    )(tile_slot, tile_list, q_model, rec_index, traces, adj_now, adj_prev, fwd_lap, mats)


def solution(mesh):
    in_specs = (
        P("shot", "sub", None),
        P(),
        P(),
        P("shot", None),
        P("shot", None, None),
        P("shot", "sub", None),
        P("shot", "sub", None),
        P("shot", None, "sub", None),
    )
    out_specs = (P("shot", "sub", None), P("shot", "sub", None))
    return jax.shard_map(body, mesh=mesh, in_specs=in_specs, out_specs=out_specs, check_vma=False)
```

time: 739 us -> 105 us (0.14)
  the two profiles are of different devices: /device:TPU:1 before, /device:TPU:32 now
where the time goes in v2:
time: 105 us
  Pallas kernels  99.3 us (95%)
  local copies, waits for them, and re-layouts  4.63 us (4%)
    pallas_call x1, Pallas kernels, body(): pl.pallas_call(kernel, out_shape=(jax.ShapeDtypeStruct((4, ROWS, LANES),...  99.3 us
    unnamed x3, local copies, waits for them, and re-layouts  4.63 us

profile of v2, /device:TPU:32, one launch (start us, length us, event | category | flops | bytes accessed | tf_op | source)
XLA Modules:
  0.0 104.6 jit_solution(3002899942474504549)
XLA Ops:
  0.6 1.4 %copy.11.tl = s32[64,16]{1,0:T(8,128)} copy(s32[64,16]{0,1:T(8,128)} %param.11) | data formatting | bytes 8192 | tf_op args[2]
  2.0 99.3 %shard_map.104 = (f32[4,32,256]{2,1,0:T(8,128)}, bf16[1,32,4096]{2,1,0:T(8,128)(2,1)}) custom-call(s32[256]{0:T(256)} %ts.1, s32[64,16]{1,0:T(8,128)} %copy.11.tl, f32[4,32,256]{2,1,0:T(8,128)} %q_ref.1, s32[1,256]{1,0:T(1,128)} %rec.1, f32[1,8,256]{2,1,0:T(8,128)} %tr.1, f32[1,32,4096]{2,1,0:T(8,128)} %u_in.1, f32[1,32,4096]{2,1,0:T(8,128)} %w_in.1, ...), custom_call_target="tpu_custom_call" | custom-call | tf_op jit(solution)/shard_map/pallas_call | solution.py:635
  101.4 1.6 %copy.14 = f32[4,32,256]{2,1,0:T(8,128)} copy(f32[4,32,256]{2,1,0:T(8,128)} %get-tuple-element.4) | data formatting | bytes 262144
  102.9 1.7 %copy.15 = bf16[1,32,4096]{2,1,0:T(8,128)(2,1)} copy(bf16[1,32,4096]{2,1,0:T(8,128)(2,1)} %get-tuple-element.5) | data formatting | bytes 524288

commit v3 on v2

--- a/solution.py
+++ b/solution.py
@@ -45,13 +45,13 @@
 
 
 def ring(v):
-    return (v + 8) % 4
+    return (v + 8) & 3
 
 
 class Links:
     def __init__(self):
         me = lax.axis_index("shot")
-        self.at = {"y": me // 16, "x": (me // 4) % 4, "z": me % 4}
+        self.at = {"y": me >> 4, "x": (me >> 2) & 3, "z": me & 3}
         self.shot = me
         self.sub = lax.axis_index("sub")
 
@@ -77,14 +77,16 @@
 
 def slot_parts(slot, order):
     if order == 0:
-        return slot // 64, slot % 64
-    return (slot // 16) % 4, (slot // 64) * 16 + slot % 16
+        return slot >> 6, slot & 63
+    return (slot >> 4) & 3, ((slot >> 6) << 4) + (slot & 15)
 
 
 class Gather:
-    def __init__(self, links, ts, tl, q_ref, QF, g, rel_s, rel_r, blk_s, blk_r, sems):
+    def __init__(self, links, ts, tl, q_ref, QF, g, rel_s, rel_r, blk_s, blk_r, own_sem, sems):
         self.links, self.ts, self.tl, self.q_ref, self.QF = links, ts, tl, q_ref, QF
         self.g, self.rel_s, self.rel_r, self.blk_s, self.blk_r = g, rel_s, rel_r, blk_s, blk_r
+        self.own_sem = own_sem
+        self.kept = {}
         self.sems = sems
         self.sent = []
         self.live = {}
@@ -109,13 +111,20 @@
         src = self.q_ref.at[:, pl.ds(c * R, R)]
         for d, delta in DIRS:
             self.go("zp1", c, d, "z", delta, src, self.part(c, line, z), 0)
+
+    def own(self, c):
+        z, line = self.links.at["z"], self.line(c)
+        src = self.q_ref.at[:, pl.ds(c * R, R)]
         for d, delta in DIRS:
             self.go("a1own", c, d, axes_of(c)[0], delta, src, self.part(c, line, z), 4)
 
     def keep(self, c):
         z, line = self.links.at["z"], self.line(c)
-        for t in range(4):
-            self.g[c][line * 16 + z * 4 + t] = self.q_ref[t, c * R : (c + 1) * R, :]
+        copy = pltpu.make_async_copy(
+            self.q_ref.at[:, pl.ds(c * R, R)], self.part(c, line, z), self.own_sem.at[c]
+        )
+        copy.start()
+        self.kept[c] = copy
 
     def zp2(self, c):
         z, line = self.links.at["z"], self.line(c)
@@ -157,11 +166,12 @@
         self.forward("a1f", "a2f", c, ring(self.links.at["z"] + 2), 18)
 
     def target(self, c, delta, p):
-        slot = self.ts[self.tl[self.links.step(axes_of(c)[1], delta), p]]
+        slot = self.ts[self.tl[p, self.links.step(axes_of(c)[1], delta)]]
         return slot_parts(slot, c % 2)
 
     def rel(self, c):
         last = axes_of(c)[1]
+        self.kept[c].wait()
         for d in range(2):
             for name in ("a2own", "a2m", "a2p", "a2f"):
                 self.got(name, c, d)
@@ -171,23 +181,36 @@
                 self.rel_s[c][d, p] = self.g[c][at]
             self.go("rel", c, d, last, delta, self.rel_s[c].at[d], self.rel_r[c].at[d], 20)
 
+    def half(self, name, c, d, delta, side, k):
+        piece = pl.ds(8 * side, 8)
+        self.go(
+            name, c, d, axes_of(c)[1], delta,
+            self.blk_s[c].at[d, piece], self.blk_r[c].at[d, piece], k,
+        )
+
+    def near(self, c):
+        for d, delta in DIRS:
+            for p in range(8 * (1 - d), 8 * (2 - d)):
+                _, at = self.target(c, delta, p)
+                self.blk_s[c][d, p] = self.g[c][at]
+            self.half("near", c, d, delta, 1 - d, 24)
+
     def blk(self, c):
-        last = axes_of(c)[1]
-        mine = self.links.at[last]
+        mine = self.links.at[axes_of(c)[1]]
         for d, delta in DIRS:
             self.got("rel", c, d)
-            for p in range(16):
+            for p in range(8 * d, 8 * (1 + d)):
                 owner, at = self.target(c, delta, p)
-                value = self.g[c][at]
-                if p // 8 == d:
-                    value = jnp.where(owner == mine, value, self.rel_r[c][d, p % 8])
-                self.blk_s[c][d, p] = value
-            self.go("blk", c, d, last, delta, self.blk_s[c].at[d], self.blk_r[c].at[d], 22)
+                self.blk_s[c][d, p] = jnp.where(
+                    owner == mine, self.g[c][at], self.rel_r[c][d, p % 8]
+                )
+            self.half("blk", c, d, delta, d, 22)
 
     def finish(self, c):
         mine = self.links.at[axes_of(c)[1]]
         blk_r = self.blk_r[c]
         for d in range(2):
+            self.got("near", c, d)
             self.got("blk", c, d)
         for p in range(16):
             owner, at = self.target(c, 0, p)
@@ -209,11 +232,12 @@
 
 class Scatter:
     def __init__(
-        self, links, tab, out_ref, gg, rel_s, rel_r, blk_s, blk_r, col, zrel_r, zblk_s, zblk_r, sems
+        self, links, tab, out_ref, GO, out_sem, gg, rel_s, rel_r, blk_s, blk_r, col, zrel_r, zblk_s, zblk_r, sems
     ):
         self.links, self.tab, self.out_ref, self.gg, self.col = links, tab, out_ref, gg, col
         self.rel_s, self.rel_r, self.blk_s, self.blk_r = rel_s, rel_r, blk_s, blk_r
         self.zrel_r, self.zblk_s, self.zblk_r = zrel_r, zblk_s, zblk_r
+        self.GO, self.out_sem, self.outs = GO, out_sem, []
         self.sems = sems
         self.sent = []
         self.live = {}
@@ -260,21 +284,31 @@
         for e in range(16):
             self.col[c][e] = self.partial(c, self.line(c), e)
 
+    def half(self, name, c, d, delta, side, k):
+        piece = pl.ds(8 * side, 8)
+        self.go(
+            name, c, d, axes_of(c)[0], delta,
+            self.blk_s[c].at[d, piece], self.blk_r[c].at[d, piece], k,
+        )
+
+    def near(self, c):
+        for d, delta in DIRS:
+            for e in range(8 * (1 - d), 8 * (2 - d)):
+                self.blk_s[c][d, e] = self.partial(c, ring(self.line(c) + delta), e)
+            self.half("near", c, d, delta, 1 - d, 14)
+
     def blk(self, c):
         for d, delta in DIRS:
             self.got("rel", c, d)
-            for e in range(16):
+            for e in range(8 * d, 8 * (1 + d)):
                 value = self.partial(c, ring(self.line(c) + delta), e)
-                if e // 8 == d:
-                    value = value + self.rel_r[c][d, e % 8]
-                self.blk_s[c][d, e] = value
-            self.go(
-                "blk", c, d, axes_of(c)[0], delta, self.blk_s[c].at[d], self.blk_r[c].at[d], 8
-            )
+                self.blk_s[c][d, e] = value + self.rel_r[c][d, e % 8]
+            self.half("blk", c, d, delta, d, 8)
 
     def zrel(self, c):
         z = self.links.at["z"]
         for d in range(2):
+            self.got("near", c, d)
             self.got("blk", c, d)
         for e in range(16):
             self.col[c][e] += self.blk_r[c][0, e] + self.blk_r[c][1, e]
@@ -282,25 +316,35 @@
             piece = self.col[c].at[pl.ds(ring(z + 2) * 4 + 2 * d, 2)]
             self.go("zrel", c, d, "z", delta, piece, self.zrel_r[c].at[d], 10)
 
+    def znear(self, c):
+        z = self.links.at["z"]
+        for d, delta in DIRS:
+            piece = self.col[c].at[pl.ds(ring(z + delta) * 4 + 2 * (1 - d), 2)]
+            home = self.zblk_r[c].at[d, pl.ds(2 * (1 - d), 2)]
+            self.go("znear", c, d, "z", delta, piece, home, 16)
+
     def zblk(self, c):
         z = self.links.at["z"]
         for d, delta in DIRS:
             self.got("zrel", c, d)
-            for t in range(4):
-                value = self.col[c][ring(z + delta) * 4 + t]
-                if t // 2 == d:
-                    value = value + self.zrel_r[c][d, t % 2]
-                self.zblk_s[c][d, t] = value
-            self.go("zblk", c, d, "z", delta, self.zblk_s[c].at[d], self.zblk_r[c].at[d], 12)
+            for t in range(2):
+                value = self.col[c][ring(z + delta) * 4 + 2 * d + t]
+                self.zblk_s[c][d, t] = value + self.zrel_r[c][d, t]
+            home = self.zblk_r[c].at[d, pl.ds(2 * d, 2)]
+            self.go("zblk", c, d, "z", delta, self.zblk_s[c].at[d], home, 12)
 
     def finish(self, c):
         z = self.links.at["z"]
         for d in range(2):
+            self.got("znear", c, d)
             self.got("zblk", c, d)
         for t in range(4):
-            self.out_ref[t, c * R : (c + 1) * R, :] = (
-                self.col[c][z * 4 + t] + self.zblk_r[c][0, t] + self.zblk_r[c][1, t]
-            )
+            self.GO[c][t] = self.col[c][z * 4 + t] + self.zblk_r[c][0, t] + self.zblk_r[c][1, t]
+        copy = pltpu.make_async_copy(
+            self.GO[c], self.out_ref.at[:, pl.ds(c * R, R)], self.out_sem.at[c]
+        )
+        copy.start()
+        self.outs.append(copy)
 
 
 def split2(v):
@@ -320,7 +364,7 @@
     return lax.dot_general(a, b, dims, preferred_element_type=F32)
 
 
-def kernel(ts, tl, q_ref, rec, tr, u_in, w_in, fwd, mats, grad_out, fin_out, *scratch):
+def kernel(ts, tl, q_ref, rec, tr, u_hbm, w_hbm, fwd, mats_hbm, grad_out, fin_out, *scratch):
     scratch = list(scratch)
 
     def take(n):
@@ -328,18 +372,22 @@
         del scratch[:n]
         return out
 
-    U, H, LO, ACC, Q, G, S, PM, QF, T3, FW, hs, hr, tabv, tab = take(15)
+    U, H, LO, ACC, Q, G, S, PM, QF, T3, FW, hs, hr, tabv, tab, u_in, w_in, mats, FO = take(19)
     g, rel_s, rel_r, blk_s, blk_r = (take(NCH) for _ in range(5))
     gg, grel_s, grel_r, gblk_s, gblk_r = (take(NCH) for _ in range(5))
-    col, zrel_r, zblk_s, zblk_r = (take(NCH) for _ in range(4))
-    ssem, rsem, qs, qr, gs, gr, lsem = take(7)
+    col, zrel_r, zblk_s, zblk_r, GO = (take(NCH) for _ in range(5))
+    ssem, rsem, qs, qr, gs, gr, lsem, own_sem, out_sem = take(9)
 
     links = Links()
     shot, sub = links.shot, links.sub
     has_up, has_dn = sub > 0, sub < 3
     sides = ((has_up, sub - 1), (has_dn, sub + 1))
-    load = pltpu.make_async_copy(fwd.at[0], FW, lsem.at[0])
-    load.start()
+    loads = [
+        pltpu.make_async_copy(src, dst, lsem.at[k])
+        for k, (src, dst) in enumerate(
+            ((u_hbm, u_in), (w_hbm, w_in), (mats_hbm, mats), (fwd.at[0], FW))
+        )
+    ]
 
     sem = pltpu.get_barrier_semaphore()
     for axis in ("y", "x", "z"):
@@ -402,6 +450,9 @@
             H[32 + 32 * j : 64 + 32 * j, :] = hi
             LO[32 + 32 * j : 64 + 32 * j, :] = lo
         G[...] = jnp.zeros(G.shape, F32)
+        tabv[...] = jnp.full((8, 128), 64, jnp.int32)
+        for c in range(NCH):
+            gg[c][64] = jnp.zeros((R, LANES), F32)
 
     receivers = rec[...]
     column = receivers & (PLANE - 1)
@@ -434,66 +485,85 @@
         moved = ((src >> 4) & 7) * 64 + (src >> 7) * 16 + (src & 15)
         PM[...] = (moved == dst).astype(F32).astype(BF16)
 
-    def table():
+    def table_rows(acc, p):
         row_at = lax.broadcasted_iota(jnp.int32, (8, 128), 0)
         lane_at = lax.broadcasted_iota(jnp.int32, (8, 128), 1)
-
-        def table_row(p, acc):
-            for order in range(2):
-                first = ("y", "x")[order]
-                m = links.at[first]
-                for src in range(4):
-                    slot = ts[tl[links.step(first, src - m), p]]
-                    owner, at = slot_parts(slot, order)
-                    at = jnp.where(owner == m, at, -1)
-                    hit = (row_at == order * 4 + src) & (lane_at == at)
-                    acc = jnp.where(hit, src * 16 + p, acc)
-            return acc
-
-        tabv[...] = lax.fori_loop(0, 16, table_row, jnp.full((8, 128), 64, jnp.int32))
-        for c in range(NCH):
-            gg[c][64] = jnp.zeros((R, LANES), F32)
-
-    gather = Gather(links, ts, tl, q_ref, QF, g, rel_s, rel_r, blk_s, blk_r, (qs, qr))
-    A, B = (0, 1), (2, 3)
-
-    def each(step, chunks):
-        for c in chunks:
-            step(c)
-
-    each(gather.start, A)
-    each(gather.start, B)
-    init_fields()
-    each(gather.keep, A + B)
-    each(gather.zp2, A)
-    each(gather.a1n, A)
-    each(gather.a2own, A)
+        for order in range(2):
+            first = ("y", "x")[order]
+            m = links.at[first]
+            for src in range(4):
+                slot = ts[tl[p, links.step(first, src - m)]]
+                owner, at = slot_parts(slot, order)
+                at = jnp.where(owner == m, at, -1)
+                hit = (row_at == order * 4 + src) & (lane_at == at)
+                acc = jnp.where(hit, src * 16 + p, acc)
+        return acc
+
+    gather = Gather(links, ts, tl, q_ref, QF, g, rel_s, rel_r, blk_s, blk_r, own_sem, (qs, qr))
+    every = range(NCH)
+    gather.start(0)
+    gather.start(1)
+    for copy in loads:
+        copy.start()
+    gather.own(0)
+    gather.own(1)
+    gather.start(2)
+    gather.own(2)
+    gather.start(3)
+    gather.own(3)
+    for c in every:
+        gather.keep(c)
     source_values()
     sources(0, 4)
-    each(gather.zp2, B)
-    each(gather.a1f, A)
-    each(gather.a1n, B)
-    each(gather.a2n, A)
-    each(gather.a2own, B)
+    permutation()
+    gather.zp2(0)
+    gather.a2own(0)
+    gather.a2own(1)
+    gather.zp2(1)
+    gather.a1n(1)
+    gather.a1n(0)
     sources(4, 8)
-    each(gather.a2f, A)
-    each(gather.a1f, B)
-    each(gather.a2n, B)
+    gather.zp2(2)
+    loads[0].wait()
+    loads[1].wait()
+    init_fields()
+    gather.a1n(2)
+    gather.zp2(3)
+    gather.a1n(3)
     sources(8, 12)
-    each(gather.rel, A)
-    each(gather.a2f, B)
+    gather.a1f(0)
+    gather.a1f(1)
+    gather.a2n(1)
+    gather.a1f(2)
+    gather.a2n(0)
+    gather.a1f(3)
+    gather.a2f(0)
+    gather.a2f(1)
+    gather.a2n(3)
+    gather.a2own(3)
+    gather.a2own(2)
     sources(12, 16)
-    each(gather.blk, A)
-    permutation()
-    each(gather.rel, B)
-    table()
-    fill = pltpu.make_async_copy(tabv, tab, lsem.at[1])
-    fill.start()
-    each(gather.finish, A)
-    each(gather.blk, B)
-    fill.wait()
-    load.wait()
-    each(gather.finish, B)
+    gather.a2f(2)
+    gather.a2n(2)
+    gather.a2f(3)
+    gather.rel(0)
+    gather.rel(1)
+    gather.near(1)
+    gather.near(0)
+    gather.rel(2)
+    gather.rel(3)
+    gather.near(2)
+    gather.near(3)
+    gather.blk(0)
+    gather.blk(1)
+    gather.blk(2)
+    gather.blk(3)
+    gather.finish(0)
+    gather.finish(1)
+    gather.finish(2)
+    gather.finish(3)
+    loads[2].wait()
+    loads[3].wait()
     gather.drain()
 
     for k in range(8):
@@ -512,6 +582,7 @@
             [buf[32 * d : 32 * d + 512, :] for buf in (H, LO) for d in range(3)], axis=1
         )
         ACC[...] = dot(wide, mats[...])
+        tabv[...] = table_rows(table_rows(tabv[...], 2 * t), 2 * t + 1)
         for c in range(HC):
             for side in range(2):
 
@@ -552,9 +623,11 @@
         return carry
 
     lax.fori_loop(0, STEPS, one_step, 0)
+    fill = pltpu.make_async_copy(tabv, tab, lsem.at[4])
+    fill.start()
 
     scatter = Scatter(
-        links, tab, grad_out, gg, grel_s, grel_r, gblk_s, gblk_r, col, zrel_r, zblk_s, zblk_r, (gs, gr)
+        links, tab, grad_out, GO, out_sem, gg, grel_s, grel_r, gblk_s, gblk_r, col, zrel_r, zblk_s, zblk_r, (gs, gr)
     )
     for k in range(8):
         wide = jnp.concatenate([G[2 * k], G[2 * k + 1]], axis=1)
@@ -572,35 +645,70 @@
                     gg[c][at, :, 128 * h : 128 * h + 128] = total[
                         row : row + R, 128 * b : 128 * b + 128
                     ]
-    for c in A:
-        scatter.a1(c, 0)
-        scatter.a1(c, 1)
-    for c in B:
-        scatter.a1(c, 0)
+    scatter.a1(3, 0)
+    scatter.a1(1, 0)
+    scatter.a1(3, 1)
+    scatter.a1(2, 0)
+    scatter.a1(0, 0)
+    scatter.a1(2, 1)
+    scatter.a1(1, 1)
     for cb in range(32):
-        fin_out[0, :, cb * 128 : (cb + 1) * 128] = U[STEPS % 2, cb, 8:40, :].astype(BF16)
-    each(scatter.a2, A)
-    for c in B:
-        scatter.a1(c, 1)
-    each(scatter.a2, B)
-    each(scatter.rel, A)
-    each(scatter.own, A)
-    each(scatter.blk, A)
-    each(scatter.rel, B)
-    each(scatter.own, B)
-    each(scatter.zrel, A)
-    each(scatter.blk, B)
-    each(scatter.zblk, A)
-    each(scatter.finish, A)
-    each(scatter.zrel, B)
-    each(scatter.zblk, B)
-    each(scatter.finish, B)
+        FO[0, :, cb * 128 : (cb + 1) * 128] = U[STEPS % 2, cb, 8:40, :].astype(BF16)
+    final = pltpu.make_async_copy(FO, fin_out, out_sem.at[NCH])
+    final.start()
+    fill.wait()
+    scatter.a2(3)
+    scatter.a2(2)
+    scatter.a2(0)
+    scatter.a1(0, 1)
+    scatter.a2(1)
+    scatter.rel(2)
+    scatter.rel(3)
+    scatter.near(2)
+    scatter.near(3)
+    scatter.rel(0)
+    scatter.rel(1)
+    scatter.blk(2)
+    scatter.own(3)
+    scatter.blk(3)
+    scatter.own(0)
+    scatter.near(0)
+    scatter.near(1)
+    scatter.own(2)
+    scatter.blk(0)
+    scatter.own(1)
+    scatter.zrel(2)
+    scatter.blk(1)
+    scatter.znear(2)
+    scatter.zrel(3)
+    scatter.znear(3)
+    scatter.zrel(0)
+    scatter.zblk(2)
+    scatter.zrel(1)
+    scatter.znear(1)
+    scatter.znear(0)
+    scatter.zblk(0)
+    scatter.zblk(3)
+    scatter.zblk(1)
+    scatter.finish(0)
+    scatter.finish(2)
+    scatter.finish(3)
+    scatter.finish(1)
     scatter.drain()
+    final.wait()
+    for copy in scatter.outs:
+        copy.wait()
+
+
+def hand_over(grad, final, grad_out, fin_out):
+    grad_out[...] = grad[...]
+    fin_out[...] = final[...]
 
 
 def body(q_model, tile_slot, tile_list, rec_index, traces, adj_now, adj_prev, fwd_lap):
     smem = pl.BlockSpec(memory_space=pltpu.SMEM)
     vmem = pl.BlockSpec(memory_space=pltpu.VMEM)
+    hbm = pl.BlockSpec(memory_space=pl.ANY)
     mats = jnp.asarray(lateral_matrices(), BF16)
     scratch = [
         pltpu.VMEM((2, 32, 48, 128), F32),
@@ -618,6 +726,10 @@
         pltpu.VMEM((2, 2, HC, CB, 4, 128), F32),
         pltpu.VMEM((8, 128), jnp.int32),
         pltpu.SMEM((8, 128), jnp.int32),
+        pltpu.VMEM((1, ROWS, PLANE), F32),
+        pltpu.VMEM((1, ROWS, PLANE), F32),
+        pltpu.VMEM((6 * LANES, LANES), BF16),
+        pltpu.VMEM((1, ROWS, PLANE), BF16),
     ]
     scratch += [pltpu.VMEM((64, R, LANES), F32)] * NCH
     scratch += [pltpu.VMEM((2, 8, R, LANES), F32)] * (2 * NCH)
@@ -627,24 +739,36 @@
     scratch += [pltpu.VMEM((2, 16, R, LANES), F32)] * (2 * NCH)
     scratch += [pltpu.VMEM((16, R, LANES), F32)] * NCH
     scratch += [pltpu.VMEM((2, 2, R, LANES), F32)] * NCH
-    scratch += [pltpu.VMEM((2, 4, R, LANES), F32)] * (2 * NCH)
+    scratch += [pltpu.VMEM((2, 2, R, LANES), F32)] * NCH
+    scratch += [pltpu.VMEM((2, 4, R, LANES), F32)] * NCH
+    scratch += [pltpu.VMEM((4, R, LANES), F32)] * NCH
     scratch += [pltpu.SemaphoreType.DMA((2, 2, HC))] * 2
-    scratch += [pltpu.SemaphoreType.DMA((NCH, 24))] * 2
-    scratch += [pltpu.SemaphoreType.DMA((NCH, 14))] * 2
-    scratch += [pltpu.SemaphoreType.DMA((2,))]
-    return pl.pallas_call(
+    scratch += [pltpu.SemaphoreType.DMA((NCH, 26))] * 2
+    scratch += [pltpu.SemaphoreType.DMA((NCH, 18))] * 2
+    scratch += [pltpu.SemaphoreType.DMA((5,)), pltpu.SemaphoreType.DMA((NCH,))]
+    scratch += [pltpu.SemaphoreType.DMA((NCH + 1,))]
+    grad, final = pl.pallas_call(
         kernel,
         out_shape=(
             jax.ShapeDtypeStruct((4, ROWS, LANES), F32),
             jax.ShapeDtypeStruct((1, ROWS, PLANE), BF16),
         ),
-        in_specs=[smem, smem] + [vmem] * 5 + [pl.BlockSpec(memory_space=pl.ANY), vmem],
-        out_specs=(vmem, vmem),
+        in_specs=[smem, smem, hbm, vmem, vmem] + [hbm] * 4,
+        out_specs=(hbm, hbm),
         scratch_shapes=scratch,
         compiler_params=pltpu.CompilerParams(
             collective_id=0, has_side_effects=True, vmem_limit_bytes=VMEM_LIMIT
         ),
-    )(tile_slot, tile_list, q_model, rec_index, traces, adj_now, adj_prev, fwd_lap, mats)
+    )(tile_slot, tile_list.T, q_model, rec_index, traces, adj_now, adj_prev, fwd_lap, mats)
+    return pl.pallas_call(
+        hand_over,
+        out_shape=(
+            jax.ShapeDtypeStruct(grad.shape, F32),
+            jax.ShapeDtypeStruct(final.shape, BF16),
+        ),
+        in_specs=[vmem, vmem],
+        out_specs=(vmem, vmem),
+    )(grad, final)
 
 
 def solution(mesh):

time: 105 us -> 92.2 us (0.88)
  the two profiles are of different devices: /device:TPU:32 before, /device:TPU:1 now
where the time goes in v3:
time: 92.2 us; the launch traced here: 91.5 us
  Pallas kernels  90.8 us (98%)
    pallas_call x1, Pallas kernels, body(): pl.pallas_call(kernel, out_shape=(jax.ShapeDtypeStruct((4, ROWS, LANES),...  89 us

profile of v3, /device:TPU:1, one launch (start us, length us, event | category | flops | bytes accessed | tf_op | source)
XLA Modules:
  0.0 91.5 jit_solution(4862077429029911461)
XLA Ops:
  0.6 89.0 %shard_map.104 = (f32[4,32,256]{2,1,0:T(8,128)}, bf16[1,32,4096]{2,1,0:T(8,128)(2,1)}) custom-call(s32[256]{0:T(256)} %ts.1, s32[16,64]{1,0:T(8,128)} %bitcast.1, f32[4,32,256]{2,1,0:T(8,128)} %q_ref.1, s32[1,256]{1,0:T(1,128)} %rec.1, f32[1,8,256]{2,1,0:T(8,128)} %tr.1, f32[1,32,4096]{2,1,0:T(8,128)} %u_hbm.1, f32[1,32,4096]{2,1,0:T(8,128)} %w_hbm.1, ...), custom_call_target="tpu_custom_call" | custom-call | tf_op jit(solution)/shard_map/pallas_call | solution.py:750
  89.7 1.8 %shard_map.105 = (f32[4,32,256]{2,1,0:T(8,128)}, bf16[1,32,4096]{2,1,0:T(8,128)(2,1)}) custom-call(f32[4,32,256]{2,1,0:T(8,128)} %get-tuple-element.4.grad, bf16[1,32,4096]{2,1,0:T(8,128)(2,1)} %get-tuple-element.5.final), custom_call_target="tpu_custom_call" | custom-call | tf_op jit(solution)/shard_map/pallas_call | solution.py:763

commit v4 on v3

--- a/solution.py
+++ b/solution.py
@@ -107,16 +107,13 @@
         return self.g[c].at[pl.ds(line * 16 + zz * 4 + t0, n)]
 
     def start(self, c):
-        z, line = self.links.at["z"], self.line(c)
-        src = self.q_ref.at[:, pl.ds(c * R, R)]
-        for d, delta in DIRS:
-            self.go("zp1", c, d, "z", delta, src, self.part(c, line, z), 0)
+        self.kept[c].wait()
+        piece = self.part(c, self.line(c), self.links.at["z"])
+        for d, delta in DIRS:
+            self.go("zp1", c, d, "z", delta, piece, piece, 0)
 
     def own(self, c):
-        z, line = self.links.at["z"], self.line(c)
-        src = self.q_ref.at[:, pl.ds(c * R, R)]
-        for d, delta in DIRS:
-            self.go("a1own", c, d, axes_of(c)[0], delta, src, self.part(c, line, z), 4)
+        self.spread("a1own", c, self.links.at["z"], 4)
 
     def keep(self, c):
         z, line = self.links.at["z"], self.line(c)
@@ -171,7 +168,6 @@
 
     def rel(self, c):
         last = axes_of(c)[1]
-        self.kept[c].wait()
         for d in range(2):
             for name in ("a2own", "a2m", "a2p", "a2f"):
                 self.got(name, c, d)
@@ -364,7 +360,7 @@
     return lax.dot_general(a, b, dims, preferred_element_type=F32)
 
 
-def kernel(ts, tl, q_ref, rec, tr, u_hbm, w_hbm, fwd, mats_hbm, grad_out, fin_out, *scratch):
+def kernel(ts_hbm, tl_hbm, q_ref, rec_hbm, tr_hbm, u_hbm, w_hbm, fwd, mats_hbm, grad_out, fin_out, *scratch):
     scratch = list(scratch)
 
     def take(n):
@@ -372,7 +368,7 @@
         del scratch[:n]
         return out
 
-    U, H, LO, ACC, Q, G, S, PM, QF, T3, FW, hs, hr, tabv, tab, u_in, w_in, mats, FO = take(19)
+    U, H, LO, ACC, Q, G, S, PM, QF, T3, FW, hs, hr, tabv, tab, u_in, w_in, mats, FO, ts, tl, rec, tr = take(23)
     g, rel_s, rel_r, blk_s, blk_r = (take(NCH) for _ in range(5))
     gg, grel_s, grel_r, gblk_s, gblk_r = (take(NCH) for _ in range(5))
     col, zrel_r, zblk_s, zblk_r, GO = (take(NCH) for _ in range(5))
@@ -385,7 +381,10 @@
     loads = [
         pltpu.make_async_copy(src, dst, lsem.at[k])
         for k, (src, dst) in enumerate(
-            ((u_hbm, u_in), (w_hbm, w_in), (mats_hbm, mats), (fwd.at[0], FW))
+            (
+                (rec_hbm, rec), (tr_hbm, tr), (ts_hbm, ts), (tl_hbm, tl),
+                (u_hbm, u_in), (w_hbm, w_in), (mats_hbm, mats), (fwd.at[0], FW),
+            )
         )
     ]
 
@@ -401,7 +400,11 @@
         def _():
             pl.semaphore_signal(sem, inc=1, device_id=(shot, other), device_id_type=MESH)
 
-    pl.semaphore_wait(sem, 6 + has_up.astype(jnp.int32) + has_dn.astype(jnp.int32))
+    gather = Gather(links, ts, tl, q_ref, QF, g, rel_s, rel_r, blk_s, blk_r, own_sem, (qs, qr))
+    for c in range(NCH):
+        gather.keep(c)
+    for copy in loads:
+        copy.start()
 
     def halo(slot, side, c):
         return pltpu.make_async_remote_copy(
@@ -454,6 +457,8 @@
         for c in range(NCH):
             gg[c][64] = jnp.zeros((R, LANES), F32)
 
+    loads[0].wait()
+    loads[1].wait()
     receivers = rec[...]
     column = receivers & (PLANE - 1)
     level = (receivers >> 12) - sub * ROWS
@@ -484,6 +489,12 @@
         dst = lax.broadcasted_iota(jnp.int32, (512, 512), 1)
         moved = ((src >> 4) & 7) * 64 + (src >> 7) * 16 + (src & 15)
         PM[...] = (moved == dst).astype(F32).astype(BF16)
+
+    def lateral():
+        wide = jnp.concatenate(
+            [buf[32 * d : 32 * d + 512, :] for buf in (H, LO) for d in range(3)], axis=1
+        )
+        ACC[...] = dot(wide, mats[...])
 
     def table_rows(acc, p):
         row_at = lax.broadcasted_iota(jnp.int32, (8, 128), 0)
@@ -499,23 +510,19 @@
                 acc = jnp.where(hit, src * 16 + p, acc)
         return acc
 
-    gather = Gather(links, ts, tl, q_ref, QF, g, rel_s, rel_r, blk_s, blk_r, own_sem, (qs, qr))
+    source_values()
+    permutation()
+    pl.semaphore_wait(sem, 6 + has_up.astype(jnp.int32) + has_dn.astype(jnp.int32))
     every = range(NCH)
     gather.start(0)
     gather.start(1)
-    for copy in loads:
-        copy.start()
     gather.own(0)
     gather.own(1)
     gather.start(2)
     gather.own(2)
     gather.start(3)
     gather.own(3)
-    for c in every:
-        gather.keep(c)
-    source_values()
     sources(0, 4)
-    permutation()
     gather.zp2(0)
     gather.a2own(0)
     gather.a2own(1)
@@ -524,9 +531,11 @@
     gather.a1n(0)
     sources(4, 8)
     gather.zp2(2)
-    loads[0].wait()
-    loads[1].wait()
+    loads[4].wait()
+    loads[5].wait()
     init_fields()
+    loads[6].wait()
+    lateral()
     gather.a1n(2)
     gather.zp2(3)
     gather.a1n(3)
@@ -546,6 +555,8 @@
     gather.a2f(2)
     gather.a2n(2)
     gather.a2f(3)
+    loads[2].wait()
+    loads[3].wait()
     gather.rel(0)
     gather.rel(1)
     gather.near(1)
@@ -562,27 +573,21 @@
     gather.finish(1)
     gather.finish(2)
     gather.finish(3)
-    loads[2].wait()
-    loads[3].wait()
+    loads[7].wait()
     gather.drain()
 
     for k in range(8):
-        for s, v in enumerate(split3(QF[32 * k : 32 * k + 32, :])):
+        for s, v in enumerate(split2(QF[32 * k : 32 * k + 32, :])):
             T3[s, 32 * k : 32 * k + 32, :] = v
     for n in range(2):
         perm = PM[:, LANES * n : LANES * n + LANES]
-        total = dot(T3[0], perm) + dot(T3[1], perm) + dot(T3[2], perm)
+        total = dot(T3[0], perm) + dot(T3[1], perm)
         for k in range(8):
             Q[2 * k + n] = total[32 * k : 32 * k + 32]
 
     def one_step(t, carry):
         par = lax.rem(t, 2)
         nxt = 1 - par
-        wide = jnp.concatenate(
-            [buf[32 * d : 32 * d + 512, :] for buf in (H, LO) for d in range(3)], axis=1
-        )
-        ACC[...] = dot(wide, mats[...])
-        tabv[...] = table_rows(table_rows(tabv[...], 2 * t), 2 * t + 1)
         for c in range(HC):
             for side in range(2):
 
@@ -620,10 +625,12 @@
                 def _():
                     halo(nxt, side, c).start()
 
+        pl.when(t < STEPS - 1)(lateral)
+        tabv[...] = table_rows(table_rows(tabv[...], 2 * t), 2 * t + 1)
         return carry
 
     lax.fori_loop(0, STEPS, one_step, 0)
-    fill = pltpu.make_async_copy(tabv, tab, lsem.at[4])
+    fill = pltpu.make_async_copy(tabv, tab, lsem.at[8])
     fill.start()
 
     scatter = Scatter(
@@ -631,11 +638,11 @@
     )
     for k in range(8):
         wide = jnp.concatenate([G[2 * k], G[2 * k + 1]], axis=1)
-        for s, v in enumerate(split3(wide)):
+        for s, v in enumerate(split2(wide)):
             T3[s, 32 * k : 32 * k + 32, :] = v
     for n in range(2):
         perm = PM[LANES * n : LANES * n + LANES, :]
-        total = dot(T3[0], perm, True) + dot(T3[1], perm, True) + dot(T3[2], perm, True)
+        total = dot(T3[0], perm, True) + dot(T3[1], perm, True)
         for k in range(8):
             a, h = k // 2, k % 2
             for b in range(2):
@@ -645,55 +652,55 @@
                     gg[c][at, :, 128 * h : 128 * h + 128] = total[
                         row : row + R, 128 * b : 128 * b + 128
                     ]
+    scatter.a1(1, 0)
+    scatter.a1(0, 0)
+    scatter.a1(2, 0)
     scatter.a1(3, 0)
-    scatter.a1(1, 0)
     scatter.a1(3, 1)
-    scatter.a1(2, 0)
-    scatter.a1(0, 0)
-    scatter.a1(2, 1)
-    scatter.a1(1, 1)
+    scatter.a1(0, 1)
     for cb in range(32):
         FO[0, :, cb * 128 : (cb + 1) * 128] = U[STEPS % 2, cb, 8:40, :].astype(BF16)
     final = pltpu.make_async_copy(FO, fin_out, out_sem.at[NCH])
     final.start()
     fill.wait()
+    scatter.a2(0)
+    scatter.a1(1, 1)
+    scatter.a1(2, 1)
+    scatter.a2(1)
     scatter.a2(3)
     scatter.a2(2)
-    scatter.a2(0)
-    scatter.a1(0, 1)
-    scatter.a2(1)
-    scatter.rel(2)
-    scatter.rel(3)
-    scatter.near(2)
-    scatter.near(3)
     scatter.rel(0)
     scatter.rel(1)
+    scatter.near(0)
+    scatter.own(0)
+    scatter.rel(3)
+    scatter.rel(2)
+    scatter.blk(0)
+    scatter.near(1)
+    scatter.near(2)
+    scatter.blk(1)
+    scatter.near(3)
+    scatter.blk(3)
     scatter.blk(2)
+    scatter.zrel(0)
+    scatter.own(2)
+    scatter.znear(0)
+    scatter.own(1)
     scatter.own(3)
-    scatter.blk(3)
-    scatter.own(0)
-    scatter.near(0)
-    scatter.near(1)
-    scatter.own(2)
-    scatter.blk(0)
-    scatter.own(1)
+    scatter.zrel(1)
+    scatter.znear(1)
     scatter.zrel(2)
-    scatter.blk(1)
     scatter.znear(2)
     scatter.zrel(3)
+    scatter.zblk(0)
+    scatter.zblk(1)
     scatter.znear(3)
-    scatter.zrel(0)
     scatter.zblk(2)
-    scatter.zrel(1)
-    scatter.znear(1)
-    scatter.znear(0)
-    scatter.zblk(0)
     scatter.zblk(3)
-    scatter.zblk(1)
+    scatter.finish(2)
     scatter.finish(0)
-    scatter.finish(2)
+    scatter.finish(1)
     scatter.finish(3)
-    scatter.finish(1)
     scatter.drain()
     final.wait()
     for copy in scatter.outs:
@@ -706,7 +713,6 @@
 
 
 def body(q_model, tile_slot, tile_list, rec_index, traces, adj_now, adj_prev, fwd_lap):
-    smem = pl.BlockSpec(memory_space=pltpu.SMEM)
     vmem = pl.BlockSpec(memory_space=pltpu.VMEM)
     hbm = pl.BlockSpec(memory_space=pl.ANY)
     mats = jnp.asarray(lateral_matrices(), BF16)
@@ -730,6 +736,10 @@
         pltpu.VMEM((1, ROWS, PLANE), F32),
         pltpu.VMEM((6 * LANES, LANES), BF16),
         pltpu.VMEM((1, ROWS, PLANE), BF16),
+        pltpu.SMEM((256,), jnp.int32),
+        pltpu.SMEM((16, 64), jnp.int32),
+        pltpu.VMEM((1, LANES), jnp.int32),
+        pltpu.VMEM((1, STEPS, LANES), F32),
     ]
     scratch += [pltpu.VMEM((64, R, LANES), F32)] * NCH
     scratch += [pltpu.VMEM((2, 8, R, LANES), F32)] * (2 * NCH)
@@ -745,7 +755,7 @@
     scratch += [pltpu.SemaphoreType.DMA((2, 2, HC))] * 2
     scratch += [pltpu.SemaphoreType.DMA((NCH, 26))] * 2
     scratch += [pltpu.SemaphoreType.DMA((NCH, 18))] * 2
-    scratch += [pltpu.SemaphoreType.DMA((5,)), pltpu.SemaphoreType.DMA((NCH,))]
+    scratch += [pltpu.SemaphoreType.DMA((9,)), pltpu.SemaphoreType.DMA((NCH,))]
     scratch += [pltpu.SemaphoreType.DMA((NCH + 1,))]
     grad, final = pl.pallas_call(
         kernel,
@@ -753,7 +763,7 @@
             jax.ShapeDtypeStruct((4, ROWS, LANES), F32),
             jax.ShapeDtypeStruct((1, ROWS, PLANE), BF16),
         ),
-        in_specs=[smem, smem, hbm, vmem, vmem] + [hbm] * 4,
+        in_specs=[hbm] * 9,
         out_specs=(hbm, hbm),
         scratch_shapes=scratch,
         compiler_params=pltpu.CompilerParams(

time: 92.2 us -> 89.5 us (0.971)
  Pallas kernels: 90.8 us -> 88.8 us
    pallas_call x1, Pallas kernels: 89 us -> 87 us  [body(): pl.pallas_call(kernel, out_shape=(jax.ShapeDtypeStruct((4, ROWS, LANES),...]
where the time goes in v4:
time: 89.5 us; the launch traced here: 89.4 us
  Pallas kernels  88.8 us (99%)
    pallas_call x1, Pallas kernels, body(): pl.pallas_call(kernel, out_shape=(jax.ShapeDtypeStruct((4, ROWS, LANES),...  87 us

profile of v4, /device:TPU:1, one launch (start us, length us, event | category | flops | bytes accessed | tf_op | source)
XLA Modules:
  0.0 89.4 jit_solution(6656160234618975363)
XLA Ops:
  0.6 87.0 %shard_map.104 = (f32[4,32,256]{2,1,0:T(8,128)}, bf16[1,32,4096]{2,1,0:T(8,128)(2,1)}) custom-call(s32[256]{0:T(256)} %ts_hbm.1, s32[16,64]{1,0:T(8,128)} %bitcast.1, f32[4,32,256]{2,1,0:T(8,128)} %q_ref.1, s32[1,256]{1,0:T(1,128)} %rec_hbm.1, f32[1,8,256]{2,1,0:T(8,128)} %tr_hbm.1, f32[1,32,4096]{2,1,0:T(8,128)} %u_hbm.1, f32[1,32,4096]{2,1,0:T(8,128)} %w_hbm.1, ...), custom_call_target="tpu_custom_call" | custom-call | tf_op jit(solution)/shard_map/pallas_call | solution.py:760
  87.7 1.8 %shard_map.105 = (f32[4,32,256]{2,1,0:T(8,128)}, bf16[1,32,4096]{2,1,0:T(8,128)(2,1)}) custom-call(f32[4,32,256]{2,1,0:T(8,128)} %get-tuple-element.4.grad, bf16[1,32,4096]{2,1,0:T(8,128)(2,1)} %get-tuple-element.5.final), custom_call_target="tpu_custom_call" | custom-call | tf_op jit(solution)/shard_map/pallas_call | solution.py:773

commit v5 on v4

--- a/solution.py
+++ b/solution.py
@@ -82,10 +82,11 @@
 
 
 class Gather:
-    def __init__(self, links, ts, tl, q_ref, QF, g, rel_s, rel_r, blk_s, blk_r, own_sem, sems):
+    def __init__(self, links, ts, tl, where, q_ref, QF, g, rel_s, rel_r, blk_s, blk_r, own_sem, sems):
         self.links, self.ts, self.tl, self.q_ref, self.QF = links, ts, tl, q_ref, QF
         self.g, self.rel_s, self.rel_r, self.blk_s, self.blk_r = g, rel_s, rel_r, blk_s, blk_r
         self.own_sem = own_sem
+        self.where = where
         self.kept = {}
         self.sems = sems
         self.sent = []
@@ -163,8 +164,19 @@
         self.forward("a1f", "a2f", c, ring(self.links.at["z"] + 2), 18)
 
     def target(self, c, delta, p):
-        slot = self.ts[self.tl[p, self.links.step(axes_of(c)[1], delta)]]
-        return slot_parts(slot, c % 2)
+        both = self.where[(c % 2) * 4 + delta % 4, p]
+        return both >> 6, both & 63
+
+    def targets(self):
+        def fill(p, carry):
+            for order in range(2):
+                for delta in range(4):
+                    slot = self.ts[self.tl[p, self.links.step(("y", "x")[order], delta)]]
+                    owner, at = slot_parts(slot, order)
+                    self.where[order * 4 + delta, p] = (owner << 6) + at
+            return carry
+
+        lax.fori_loop(0, 16, fill, 0)
 
     def rel(self, c):
         last = axes_of(c)[1]
@@ -368,7 +380,7 @@
         del scratch[:n]
         return out
 
-    U, H, LO, ACC, Q, G, S, PM, QF, T3, FW, hs, hr, tabv, tab, u_in, w_in, mats, FO, ts, tl, rec, tr = take(23)
+    U, H, LO, ACC, Q, G, S, PM, QF, T3, FW, hs, hr, tabv, tab, u_in, w_in, mats, FO, ts, tl, rec, tr, where = take(24)
     g, rel_s, rel_r, blk_s, blk_r = (take(NCH) for _ in range(5))
     gg, grel_s, grel_r, gblk_s, gblk_r = (take(NCH) for _ in range(5))
     col, zrel_r, zblk_s, zblk_r, GO = (take(NCH) for _ in range(5))
@@ -400,7 +412,7 @@
         def _():
             pl.semaphore_signal(sem, inc=1, device_id=(shot, other), device_id_type=MESH)
 
-    gather = Gather(links, ts, tl, q_ref, QF, g, rel_s, rel_r, blk_s, blk_r, own_sem, (qs, qr))
+    gather = Gather(links, ts, tl, where, q_ref, QF, g, rel_s, rel_r, blk_s, blk_r, own_sem, (qs, qr))
     for c in range(NCH):
         gather.keep(c)
     for copy in loads:
@@ -522,6 +534,9 @@
     gather.own(2)
     gather.start(3)
     gather.own(3)
+    loads[2].wait()
+    loads[3].wait()
+    gather.targets()
     sources(0, 4)
     gather.zp2(0)
     gather.a2own(0)
@@ -555,8 +570,6 @@
     gather.a2f(2)
     gather.a2n(2)
     gather.a2f(3)
-    loads[2].wait()
-    loads[3].wait()
     gather.rel(0)
     gather.rel(1)
     gather.near(1)
@@ -740,6 +753,7 @@
         pltpu.SMEM((16, 64), jnp.int32),
         pltpu.VMEM((1, LANES), jnp.int32),
         pltpu.VMEM((1, STEPS, LANES), F32),
+        pltpu.SMEM((8, 16), jnp.int32),
     ]
     scratch += [pltpu.VMEM((64, R, LANES), F32)] * NCH
     scratch += [pltpu.VMEM((2, 8, R, LANES), F32)] * (2 * NCH)

time: 89.5 us -> 89.4 us (level)
  no operation moved by 1% of the time
where the time goes in v5:
time: 89.4 us; the launch traced here: 89.3 us
  Pallas kernels  88.7 us (99%)
    pallas_call x1, Pallas kernels, body(): pl.pallas_call(kernel, out_shape=(jax.ShapeDtypeStruct((4, ROWS, LANES),...  86.9 us

profile of v5, /device:TPU:1, one launch (start us, length us, event | category | flops | bytes accessed | tf_op | source)
XLA Modules:
  0.0 89.3 jit_solution(8643211947929814231)
XLA Ops:
  0.6 86.9 %shard_map.104 = (f32[4,32,256]{2,1,0:T(8,128)}, bf16[1,32,4096]{2,1,0:T(8,128)(2,1)}) custom-call(s32[256]{0:T(256)} %ts_hbm.1, s32[16,64]{1,0:T(8,128)} %bitcast.1, f32[4,32,256]{2,1,0:T(8,128)} %q_ref.1, s32[1,256]{1,0:T(1,128)} %rec_hbm.1, f32[1,8,256]{2,1,0:T(8,128)} %tr_hbm.1, f32[1,32,4096]{2,1,0:T(8,128)} %u_hbm.1, f32[1,32,4096]{2,1,0:T(8,128)} %w_hbm.1, ...), custom_call_target="tpu_custom_call" | custom-call | tf_op jit(solution)/shard_map/pallas_call | solution.py:774
  87.6 1.8 %shard_map.105 = (f32[4,32,256]{2,1,0:T(8,128)}, bf16[1,32,4096]{2,1,0:T(8,128)(2,1)}) custom-call(f32[4,32,256]{2,1,0:T(8,128)} %get-tuple-element.4.grad, bf16[1,32,4096]{2,1,0:T(8,128)(2,1)} %get-tuple-element.5.final), custom_call_target="tpu_custom_call" | custom-call | tf_op jit(solution)/shard_map/pallas_call | solution.py:787
